TPU v7x, 128 devices: a whole 4x4x4 slice. The times are simulated.
128 devices in a mesh: dp: 16 (over x_hi, y, core), section: 8 (over x_lo, z).
Axes of the slice: x: 4 (x_hi: 2, x_lo: 2; x = x_hi * 2 + x_lo), y: 4, z: 4, core: 2. Of those that a mesh axis runs over, the one named last changes fastest.
Arguments:
- inputs: bfloat16 [2560, 8192], P('dp'), may hold values from -6 to 6
- cotangent: bfloat16 [2560, 8192], P('dp'), may hold values from -0.4375 to 0.4375
- weight_in: bfloat16 [8, 8192, 512], P('section'), may hold values from -0.0625 to 0.0625
- weight_out: bfloat16 [8, 8192, 512], P('section'), may hold values from -0.25 to 0.25
- norm_gains: float32 [8, 8192], P('section'), may hold values from 0.1 to 1.9
Outputs:
- in_grad: float32 [8, 8192, 512], P('section', 'dp')
- out_grad: float32 [8, 8192, 512], P('section', 'dp')
- gain_grad: float32 [8, 8192], P('section', 'dp')
All inputs are finite; a program needn't handle non-finite values.
Results may differ from a plain program's by a relative error of at most 0.025.
Values may be sent and summed in bfloat16 or wider, within the bound.
No kernel may reach another device: no remote copies, remote signals or barrier semaphores. Data moves between devices by JAX's collectives and lax.ppermute only.
A program may use at most 192 MiB of HBM per device.

v0:
```python
import functools

import jax
import jax.numpy as jnp
from jax import lax
from jax.experimental import pallas as pl
from jax.experimental.pallas import tpu as pltpu
from jax.sharding import Mesh
from jax.sharding import PartitionSpec as P

ROWS = 16
CHUNK = 2048
SCOPED = 6 << 20
DP = ("dp_0", "dp_1", "dp_2")
CHIPS = ("dp_0", "dp_1")
CORE = "dp_2"
EPSILON = 1e-05

VMEM = pl.BlockSpec(memory_space=pltpu.VMEM)
SMEM = pl.BlockSpec(memory_space=pltpu.SMEM)
HBM = pl.BlockSpec(memory_space=pltpu.HBM)


def row_scale_of(rows_ref, width):
    def add(k, total):
        part = rows_ref[:, pl.ds(pl.multiple_of(k * CHUNK, CHUNK), CHUNK)].astype(jnp.float32)
        return total + jnp.sum(part * part, axis=1, keepdims=True)

    total = lax.fori_loop(0, width // CHUNK, add, jnp.zeros((ROWS, 1), jnp.float32))
    return lax.rsqrt(total / width + EPSILON)


def bring_in(tick, micro, first_at, ctl_ref, flag, came_ref, source_ref, rows_ref, sem):
    low = tick - first_at
    if not 0 <= low < micro:
        rows_ref[...] = came_ref[...]
        return
    mine = ctl_ref[flag] == 1

    @pl.when(mine)
    def _():
        fetch = pltpu.make_async_copy(source_ref.at[pl.ds(low * ROWS, ROWS), :], rows_ref, sem)
        fetch.start()
        fetch.wait()

    @pl.when(jnp.logical_not(mine))
    def _():
        rows_ref[...] = came_ref[...]


def forward_body(tick, micro, ctl_ref, came_ref, source_ref, w_in_far, w_out_far, gain_ref, *rest):
    (out_ref, rows_hbm, pre_hbm, w_in_ref, w_out_ref, rows_ref, pre_buf, source_sem, rows_sem, pre_sem, load_sem) = rest[-11:]
    width, hidden = w_in_ref.shape
    steps = width // CHUNK
    starting = tick == 0

    def load(which, k):
        far, near = ((w_in_far, w_in_ref), (w_out_far, w_out_ref))[which]
        cut = pl.ds(pl.multiple_of(k * CHUNK, CHUNK), CHUNK)
        return pltpu.make_async_copy(far.at[cut, :], near.at[cut, :], load_sem.at[which, k])

    if starting:
        for which in range(2):
            for k in range(steps):
                load(which, k).start()
    slot = ctl_ref[tick]
    flag = ctl_ref.shape[0] - 2
    bring_in(tick, micro, 0, ctl_ref, flag, came_ref, source_ref, rows_ref, source_sem)
    keep_rows = pltpu.make_async_copy(rows_ref, rows_hbm.at[slot], rows_sem)
    keep_rows.start()
    row_scale = row_scale_of(rows_ref, width)

    def project(k, pre):
        if starting:
            load(0, k).wait()
        cut = pl.ds(pl.multiple_of(k * CHUNK, CHUNK), CHUNK)
        normed = rows_ref[:, cut].astype(jnp.float32) * row_scale * gain_ref[:, cut]
        return pre + jnp.dot(
            normed.astype(jnp.bfloat16), w_in_ref[cut, :], preferred_element_type=jnp.float32
        )

    pre = lax.fori_loop(0, steps, project, jnp.zeros((ROWS, hidden), jnp.float32))
    pre_buf[:, :hidden] = pre
    pre_buf[:, hidden:] = jnp.broadcast_to(row_scale, (ROWS, 128))
    keep_pre = pltpu.make_async_copy(pre_buf, pre_hbm.at[slot], pre_sem)
    keep_pre.start()
    act = (pre * jax.nn.sigmoid(pre)).astype(jnp.bfloat16)

    def expand(k, carry):
        if starting:
            load(1, k).wait()
        cut = pl.ds(pl.multiple_of(k * CHUNK, CHUNK), CHUNK)
        branch = lax.dot_general(
            act, w_out_ref[cut, :], (((1,), (1,)), ((), ())), preferred_element_type=jnp.float32
        )
        out_ref[:, cut] = (rows_ref[:, cut].astype(jnp.float32) + branch).astype(jnp.bfloat16)
        return carry

    lax.fori_loop(0, steps, expand, 0)
    keep_rows.wait()
    keep_pre.wait()


def forward_step(tick, micro, ctl, came, source, w_in, w_out, gain, stores):
    width, hidden = w_in.shape
    count = 0 if stores is None else 2
    weight = VMEM if count else HBM
    same = {3: 3, 4: 4, 6: 1, 7: 2} if count else {}
    return pl.pallas_call(
        functools.partial(forward_body, tick, micro),
        out_shape=(
            jax.ShapeDtypeStruct((ROWS, width), jnp.bfloat16),
            jax.ShapeDtypeStruct((micro + 1, ROWS, width), jnp.bfloat16),
            jax.ShapeDtypeStruct((micro + 1, ROWS, hidden + 128), jnp.float32),
            pltpu.VMEM(w_in.shape, jnp.bfloat16),
            pltpu.VMEM(w_out.shape, jnp.bfloat16),
        ),
        in_specs=[SMEM, VMEM, HBM, weight, weight, VMEM] + [HBM] * count,
        out_specs=(VMEM, HBM, HBM, VMEM, VMEM),
        scratch_shapes=[
            pltpu.VMEM((ROWS, width), jnp.bfloat16),
            pltpu.VMEM((ROWS, hidden + 128), jnp.float32),
            pltpu.SemaphoreType.DMA,
            pltpu.SemaphoreType.DMA,
            pltpu.SemaphoreType.DMA,
            pltpu.SemaphoreType.DMA((2, width // CHUNK)),
        ],
        input_output_aliases=same,
        compiler_params=pltpu.CompilerParams(vmem_limit_bytes=SCOPED),
        name="forward_step",
    )(ctl, came, source, w_in, w_out, gain, *(stores or ()))


def backward_body(tick, micro, last, ctl_ref, came_ref, source_ref, w_in_ref, w_out_ref, gain_ref, *rest):
    (out_ref, rows_hbm, pre_hbm, up_hbm, pair_hbm, _, _, up_ref, rows_buf, pre_buf, pair_buf, sems) = rest[-12:]
    width, hidden = w_in_ref.shape
    steps = width // CHUNK
    slot = ctl_ref[micro + last + tick - last]
    flag = ctl_ref.shape[0] - 1
    get_pre = pltpu.make_async_copy(pre_hbm.at[slot], pre_buf, sems.at[1])
    get_pre.start()
    get_rows = pltpu.make_async_copy(rows_hbm.at[slot], rows_buf, sems.at[2])
    get_rows.start()
    bring_in(tick, micro, last, ctl_ref, flag, came_ref, source_ref, up_ref, sems.at[4])
    keep_up = pltpu.make_async_copy(up_ref, up_hbm.at[slot], sems.at[0])
    keep_up.start()

    def project(k, total):
        cut = pl.ds(pl.multiple_of(k * CHUNK, CHUNK), CHUNK)
        return total + jnp.dot(up_ref[:, cut], w_out_ref[cut, :], preferred_element_type=jnp.float32)

    grad_act = lax.fori_loop(0, steps, project, jnp.zeros((ROWS, hidden), jnp.float32))
    get_pre.wait()
    pre = pre_buf[:, :hidden]
    row_scale = pre_buf[:, hidden : hidden + 1]
    sig = jax.nn.sigmoid(pre)
    grad_pre = grad_act * sig * (1.0 + pre * (1.0 - sig))
    pair_buf[:, :hidden] = (grad_pre * row_scale).astype(jnp.bfloat16)
    pair_buf[:, hidden:] = (pre * sig).astype(jnp.bfloat16)
    keep_pair = pltpu.make_async_copy(pair_buf, pair_hbm.at[slot], sems.at[3])
    keep_pair.start()
    grad_cut = grad_pre.astype(jnp.bfloat16)
    pull = jnp.sum(grad_cut.astype(jnp.float32) * pre, axis=1, keepdims=True)
    pull = pull * row_scale * row_scale / width
    get_rows.wait()

    def expand(k, carry):
        cut = pl.ds(pl.multiple_of(k * CHUNK, CHUNK), CHUNK)
        grad_norm = lax.dot_general(
            grad_cut, w_in_ref[cut, :], (((1,), (1,)), ((), ())), preferred_element_type=jnp.float32
        )
        out_ref[:, cut] = (
            up_ref[:, cut].astype(jnp.float32)
            + row_scale * (grad_norm * gain_ref[:, cut])
            - rows_buf[:, cut].astype(jnp.float32) * pull
        ).astype(jnp.bfloat16)
        return carry

    lax.fori_loop(0, steps, expand, 0)
    keep_up.wait()
    keep_pair.wait()


def backward_step(tick, micro, last, ctl, came, source, w_in, w_out, gain, stores, kept):
    width, hidden = w_in.shape
    count = 0 if kept is None else 2
    return pl.pallas_call(
        functools.partial(backward_body, tick, micro, last),
        out_shape=(
            jax.ShapeDtypeStruct((ROWS, width), jnp.bfloat16),
            jax.ShapeDtypeStruct((micro + 1, ROWS, width), jnp.bfloat16),
            jax.ShapeDtypeStruct((micro + 1, ROWS, hidden + 128), jnp.float32),
            jax.ShapeDtypeStruct((micro + 1, ROWS, width), jnp.bfloat16),
            jax.ShapeDtypeStruct((micro + 1, ROWS, 2 * hidden), jnp.bfloat16),
            pltpu.VMEM(w_in.shape, jnp.bfloat16),
            pltpu.VMEM(w_out.shape, jnp.bfloat16),
        ),
        in_specs=[SMEM, VMEM, HBM, VMEM, VMEM, VMEM, HBM, HBM] + [HBM] * count,
        out_specs=(VMEM, HBM, HBM, HBM, HBM, VMEM, VMEM),
        scratch_shapes=[
            pltpu.VMEM((ROWS, width), jnp.bfloat16),
            pltpu.VMEM((ROWS, width), jnp.bfloat16),
            pltpu.VMEM((ROWS, hidden + 128), jnp.float32),
            pltpu.VMEM((ROWS, 2 * hidden), jnp.bfloat16),
            pltpu.SemaphoreType.DMA((5,)),
        ],
        input_output_aliases={3: 5, 4: 6, 6: 1, 7: 2, **{8 + k: 3 + k for k in range(count)}},
        compiler_params=pltpu.CompilerParams(vmem_limit_bytes=SCOPED),
        name="backward_step",
    )(ctl, came, source, w_in, w_out, gain, *stores, *(kept or ()))


def local(inputs, cotangent, weight_in, weight_out, norm_gains):
    w_in = weight_in[0]
    w_out = weight_out[0]
    gain = norm_gains
    tokens, width = inputs.shape
    hidden = w_in.shape[1]
    micro = tokens // ROWS
    sections = lax.axis_size("section")
    last = sections - 1
    pos = lax.axis_index("section")
    chips = lax.axis_size(CHIPS)
    onward = [(i, (i + 1) % sections) for i in range(sections)]
    back = [((i + 1) % sections, i) for i in range(sections)]
    ticks = jnp.arange(micro + last)
    which = jnp.concatenate([ticks - pos, ticks - last + pos])
    slots = jnp.where((which >= 0) & (which < micro), which, micro)
    ends = jnp.stack([pos == 0, pos == last])
    ctl = jnp.concatenate([slots, ends]).astype(jnp.int32)
    ctl, w_in_near, w_out_near = lax.optimization_barrier((ctl, w_in, w_out))

    def spread(rows):
        tiles = rows.reshape(tokens, chips, -1).swapaxes(0, 1)
        return lax.all_to_all(tiles, CHIPS, split_axis=0, concat_axis=0, tiled=True)

    stores = None
    kept = None
    came = inputs[:ROWS]
    arriving = cotangent[:ROWS]
    rows_wide = None
    for tick in range(micro + 2 * last):
        if tick < micro + last:
            made, *stores, w_in_near, w_out_near = forward_step(
                tick, micro, ctl, came, inputs, w_in_near, w_out_near, gain, stores
            )
            came = lax.ppermute(made, "section", onward)
        if tick >= last:
            made, *both, w_in_near, w_out_near = backward_step(
                tick, micro, last, ctl, arriving, cotangent, w_in_near, w_out_near, gain, stores, kept
            )
            stores, kept = both[:2], both[2:]
            arriving = lax.ppermute(made, "section", back)
    rows_wide = spread(stores[0][:micro].reshape(tokens, width))
    up_wide = spread(kept[0][:micro].reshape(tokens, width)).reshape(chips * tokens, -1)
    pair = kept[1][:micro].reshape(1, tokens, 2 * hidden)
    pair_wide = lax.all_to_all(
        jnp.broadcast_to(pair, (chips, tokens, 2 * hidden)), CHIPS, split_axis=0, concat_axis=0, tiled=True
    ).reshape(chips * tokens, -1)
    rows_wide = rows_wide.reshape(chips * tokens, -1)

    def column_product(left, right):
        return lax.dot_general(
            left, right, (((0,), (0,)), ((), ())), preferred_element_type=jnp.float32
        )

    half = rows_wide.shape[1] // 2
    core = lax.axis_index(CORE)
    partial = jnp.concatenate(
        [column_product(rows_wide, pair_wide[:, :hidden]), column_product(up_wide, pair_wide[:, hidden:])],
        axis=1,
    )
    mine = lax.dynamic_slice_in_dim(partial, core * half, half, 0)
    theirs = lax.dynamic_slice_in_dim(partial, (1 - core) * half, half, 0).astype(jnp.bfloat16)
    total = mine + lax.ppermute(theirs, CORE, [(0, 1), (1, 0)]).astype(jnp.float32)
    plain = total[:, :hidden]
    low = lax.axis_index(DP) * half
    gain_cut = lax.dynamic_slice_in_dim(gain[0], low, half, 0)
    w_cut = lax.dynamic_slice_in_dim(w_in, low, half, 0).astype(jnp.float32)
    in_grad = plain * gain_cut[:, None]
    gain_grad = jnp.sum(plain * w_cut, axis=1)
    return (in_grad[None], total[None, :, hidden:], gain_grad[None])


def solution(mesh):
    finer = Mesh(
        mesh.devices.reshape(2, 4, 2, mesh.shape["section"]), ("dp_0", "dp_1", "dp_2", "section")
    )
    in_specs = (
        P(DP, None),
        P(DP, None),
        P("section", None, None),
        P("section", None, None),
        P("section", None),
    )
    out_specs = (P("section", DP, None), P("section", DP, None), P("section", DP))
    return jax.shard_map(local, mesh=finer, in_specs=in_specs, out_specs=out_specs, check_vma=False)
```

profile of v0, /device:TPU:1, one launch (start us, length us, event | category | flops | bytes accessed | tf_op | source)
XLA Modules:
  0.0 481.5 jit_solution(6403593068478486498)
XLA Ops:
  11.1 6.5 %forward_step.17 = (bf16[16,8192]{1,0:T(8,128)(2,1)S(1)}, bf16[11,16,8192]{2,1,0:T(8,128)(2,1)S(1)}, f32[11,16,640]{2,1,0:T(8,128)S(1)}, bf16[8192,512]{1,0:T(8,128)(2,1)S(1)}, bf16[8192,512]{1,0:T(8,128)(2,1)S(1)}) custom-call(s32[36]{0:T(128)S(1)} %pad_add_fusion.ctl_ref, bf16[16,8192]{1,0:T(8,128)(2,1)S(1)} %slice.28.came_ref, ...), custom_call_target="tpu_custom_call" | custom-call | tf_op jit(solution)/shard_map/forward_step/pallas_call | solution.py:109
  20.1 9.1 %collective-permute-done.came_ref = bf16[16,8192]{1,0:T(8,128)(2,1)S(1)} collective-permute-done((bf16[16,8192]{1,0:T(8,128)(2,1)S(1)}, bf16[16,8192]{1,0:T(8,128)(2,1)S(1)}, u32[]{:S(2)}, u32[]{:S(2)}) %collective-permute-start) | collective-permute-done | bytes 262176 | tf_op jit(solution)/shard_map/ppermute | solution.py:247
  29.2 5.3 %forward_step.18 = (bf16[16,8192]{1,0:T(8,128)(2,1)S(1)}, bf16[11,16,8192]{2,1,0:T(8,128)(2,1)S(1)}, f32[11,16,640]{2,1,0:T(8,128)S(1)}, bf16[8192,512]{1,0:T(8,128)(2,1)S(1)}, bf16[8192,512]{1,0:T(8,128)(2,1)S(1)}) custom-call(s32[36]{0:T(128)S(1)} %pad_add_fusion.ctl_ref, ...), custom_call_target="tpu_custom_call", output_to_operand_aliasing={{3}: (3, {}), {4}: (4, {}), {1}: (6, {}), {2}: (7, {})} | custom-call | tf_op jit(solution)/shard_map/forward_step/pallas_call | solution.py:109
  34.6 8.7 %collective-permute-done.1.came_ref = bf16[16,8192]{1,0:T(8,128)(2,1)S(1)} collective-permute-done((bf16[16,8192]{1,0:T(8,128)(2,1)S(1)}, bf16[16,8192]{1,0:T(8,128)(2,1)S(1)}, u32[]{:S(2)}, u32[]{:S(2)}) %collective-permute-start.1) | collective-permute-done | bytes 262176 | tf_op jit(solution)/shard_map/ppermute | solution.py:247
  43.3 5.3 %forward_step.19 = (bf16[16,8192]{1,0:T(8,128)(2,1)S(1)}, bf16[11,16,8192]{2,1,0:T(8,128)(2,1)S(1)}, f32[11,16,640]{2,1,0:T(8,128)S(1)}, bf16[8192,512]{1,0:T(8,128)(2,1)S(1)}, bf16[8192,512]{1,0:T(8,128)(2,1)S(1)}) custom-call(s32[36]{0:T(128)S(1)} %pad_add_fusion.ctl_ref, ...), custom_call_target="tpu_custom_call", output_to_operand_aliasing={{3}: (3, {}), {4}: (4, {}), {1}: (6, {}), {2}: (7, {})} | custom-call | tf_op jit(solution)/shard_map/forward_step/pallas_call | solution.py:109
  48.7 7.7 %collective-permute-done.2.came_ref = bf16[16,8192]{1,0:T(8,128)(2,1)S(1)} collective-permute-done((bf16[16,8192]{1,0:T(8,128)(2,1)S(1)}, bf16[16,8192]{1,0:T(8,128)(2,1)S(1)}, u32[]{:S(2)}, u32[]{:S(2)}) %collective-permute-start.2) | collective-permute-done | bytes 262176 | tf_op jit(solution)/shard_map/ppermute | solution.py:247
  56.4 5.3 %forward_step.20 = (bf16[16,8192]{1,0:T(8,128)(2,1)S(1)}, bf16[11,16,8192]{2,1,0:T(8,128)(2,1)S(1)}, f32[11,16,640]{2,1,0:T(8,128)S(1)}, bf16[8192,512]{1,0:T(8,128)(2,1)S(1)}, bf16[8192,512]{1,0:T(8,128)(2,1)S(1)}) custom-call(s32[36]{0:T(128)S(1)} %pad_add_fusion.ctl_ref, ...), custom_call_target="tpu_custom_call", output_to_operand_aliasing={{3}: (3, {}), {4}: (4, {}), {1}: (6, {}), {2}: (7, {})} | custom-call | tf_op jit(solution)/shard_map/forward_step/pallas_call | solution.py:109
  61.9 7.3 %collective-permute-done.3.came_ref = bf16[16,8192]{1,0:T(8,128)(2,1)S(1)} collective-permute-done((bf16[16,8192]{1,0:T(8,128)(2,1)S(1)}, bf16[16,8192]{1,0:T(8,128)(2,1)S(1)}, u32[]{:S(2)}, u32[]{:S(2)}) %collective-permute-start.3) | collective-permute-done | bytes 262176 | tf_op jit(solution)/shard_map/ppermute | solution.py:247
  69.2 5.3 %forward_step.21 = (bf16[16,8192]{1,0:T(8,128)(2,1)S(1)}, bf16[11,16,8192]{2,1,0:T(8,128)(2,1)S(1)}, f32[11,16,640]{2,1,0:T(8,128)S(1)}, bf16[8192,512]{1,0:T(8,128)(2,1)S(1)}, bf16[8192,512]{1,0:T(8,128)(2,1)S(1)}) custom-call(s32[36]{0:T(128)S(1)} %pad_add_fusion.ctl_ref, ...), custom_call_target="tpu_custom_call", output_to_operand_aliasing={{3}: (3, {}), {4}: (4, {}), {1}: (6, {}), {2}: (7, {})} | custom-call | tf_op jit(solution)/shard_map/forward_step/pallas_call | solution.py:109
  74.6 7.3 %collective-permute-done.4.came_ref = bf16[16,8192]{1,0:T(8,128)(2,1)S(1)} collective-permute-done((bf16[16,8192]{1,0:T(8,128)(2,1)S(1)}, bf16[16,8192]{1,0:T(8,128)(2,1)S(1)}, u32[]{:S(2)}, u32[]{:S(2)}) %collective-permute-start.4) | collective-permute-done | bytes 262176 | tf_op jit(solution)/shard_map/ppermute | solution.py:247
  81.9 5.3 %forward_step.22 = (bf16[16,8192]{1,0:T(8,128)(2,1)S(1)}, bf16[11,16,8192]{2,1,0:T(8,128)(2,1)S(1)}, f32[11,16,640]{2,1,0:T(8,128)S(1)}, bf16[8192,512]{1,0:T(8,128)(2,1)S(1)}, bf16[8192,512]{1,0:T(8,128)(2,1)S(1)}) custom-call(s32[36]{0:T(128)S(1)} %pad_add_fusion.ctl_ref, ...), custom_call_target="tpu_custom_call", output_to_operand_aliasing={{3}: (3, {}), {4}: (4, {}), {1}: (6, {}), {2}: (7, {})} | custom-call | tf_op jit(solution)/shard_map/forward_step/pallas_call | solution.py:109
  87.3 7.3 %collective-permute-done.5.came_ref = bf16[16,8192]{1,0:T(8,128)(2,1)S(1)} collective-permute-done((bf16[16,8192]{1,0:T(8,128)(2,1)S(1)}, bf16[16,8192]{1,0:T(8,128)(2,1)S(1)}, u32[]{:S(2)}, u32[]{:S(2)}) %collective-permute-start.5) | collective-permute-done | bytes 262176 | tf_op jit(solution)/shard_map/ppermute | solution.py:247
  94.6 5.3 %forward_step.23 = (bf16[16,8192]{1,0:T(8,128)(2,1)S(1)}, bf16[11,16,8192]{2,1,0:T(8,128)(2,1)S(1)}, f32[11,16,640]{2,1,0:T(8,128)S(1)}, bf16[8192,512]{1,0:T(8,128)(2,1)S(1)}, bf16[8192,512]{1,0:T(8,128)(2,1)S(1)}) custom-call(s32[36]{0:T(128)S(1)} %pad_add_fusion.ctl_ref, ...), custom_call_target="tpu_custom_call", output_to_operand_aliasing={{3}: (3, {}), {4}: (4, {}), {1}: (6, {}), {2}: (7, {})} | custom-call | tf_op jit(solution)/shard_map/forward_step/pallas_call | solution.py:109
  100.1 7.3 %collective-permute-done.6.came_ref = bf16[16,8192]{1,0:T(8,128)(2,1)S(1)} collective-permute-done((bf16[16,8192]{1,0:T(8,128)(2,1)S(1)}, bf16[16,8192]{1,0:T(8,128)(2,1)S(1)}, u32[]{:S(2)}, u32[]{:S(2)}) %collective-permute-start.6) | collective-permute-done | bytes 262176 | tf_op jit(solution)/shard_map/ppermute | solution.py:247
  107.4 5.3 %forward_step.24 = (bf16[16,8192]{1,0:T(8,128)(2,1)S(1)}, bf16[11,16,8192]{2,1,0:T(8,128)(2,1)S(1)}, f32[11,16,640]{2,1,0:T(8,128)S(1)}, bf16[8192,512]{1,0:T(8,128)(2,1)S(1)}, bf16[8192,512]{1,0:T(8,128)(2,1)S(1)}) custom-call(s32[36]{0:T(128)S(1)} %pad_add_fusion.ctl_ref, ...), custom_call_target="tpu_custom_call", output_to_operand_aliasing={{3}: (3, {}), {4}: (4, {}), {1}: (6, {}), {2}: (7, {})} | custom-call | tf_op jit(solution)/shard_map/forward_step/pallas_call | solution.py:109
  121.6 5.3 %forward_step.25 = (bf16[16,8192]{1,0:T(8,128)(2,1)S(1)}, bf16[11,16,8192]{2,1,0:T(8,128)(2,1)S(1)}, f32[11,16,640]{2,1,0:T(8,128)S(1)}, bf16[8192,512]{1,0:T(8,128)(2,1)S(1)}, bf16[8192,512]{1,0:T(8,128)(2,1)S(1)}) custom-call(s32[36]{0:T(128)S(1)} %pad_add_fusion.ctl_ref, ...), custom_call_target="tpu_custom_call", output_to_operand_aliasing={{3}: (3, {}), {4}: (4, {}), {1}: (6, {}), {2}: (7, {})} | custom-call | tf_op jit(solution)/shard_map/forward_step/pallas_call | solution.py:109
  135.7 5.3 %forward_step.26 = (bf16[16,8192]{1,0:T(8,128)(2,1)S(1)}, bf16[11,16,8192]{2,1,0:T(8,128)(2,1)S(1)}, f32[11,16,640]{2,1,0:T(8,128)S(1)}, bf16[8192,512]{1,0:T(8,128)(2,1)S(1)}, bf16[8192,512]{1,0:T(8,128)(2,1)S(1)}) custom-call(s32[36]{0:T(128)S(1)} %pad_add_fusion.ctl_ref, ...), custom_call_target="tpu_custom_call", output_to_operand_aliasing={{3}: (3, {}), {4}: (4, {}), {1}: (6, {}), {2}: (7, {})} | custom-call | tf_op jit(solution)/shard_map/forward_step/pallas_call | solution.py:109
  150.1 5.3 %forward_step.27 = (bf16[16,8192]{1,0:T(8,128)(2,1)S(1)}, bf16[11,16,8192]{2,1,0:T(8,128)(2,1)S(1)}, f32[11,16,640]{2,1,0:T(8,128)S(1)}, bf16[8192,512]{1,0:T(8,128)(2,1)S(1)}, bf16[8192,512]{1,0:T(8,128)(2,1)S(1)}) custom-call(s32[36]{0:T(128)S(1)} %pad_add_fusion.ctl_ref, ...), custom_call_target="tpu_custom_call", output_to_operand_aliasing={{3}: (3, {}), {4}: (4, {}), {1}: (6, {}), {2}: (7, {})} | custom-call | tf_op jit(solution)/shard_map/forward_step/pallas_call | solution.py:109
  164.3 5.3 %forward_step.28 = (bf16[16,8192]{1,0:T(8,128)(2,1)S(1)}, bf16[11,16,8192]{2,1,0:T(8,128)(2,1)S(1)}, f32[11,16,640]{2,1,0:T(8,128)S(1)}, bf16[8192,512]{1,0:T(8,128)(2,1)S(1)}, bf16[8192,512]{1,0:T(8,128)(2,1)S(1)}) custom-call(s32[36]{0:T(128)S(1)} %pad_add_fusion.ctl_ref, ...), custom_call_target="tpu_custom_call", output_to_operand_aliasing={{3}: (3, {}), {4}: (4, {}), {1}: (6, {}), {2}: (7, {})} | custom-call | tf_op jit(solution)/shard_map/forward_step/pallas_call | solution.py:109
  178.4 5.3 %forward_step.29 = (bf16[16,8192]{1,0:T(8,128)(2,1)S(1)}, bf16[11,16,8192]{2,1,0:T(8,128)(2,1)S(1)}, f32[11,16,640]{2,1,0:T(8,128)S(1)}, bf16[8192,512]{1,0:T(8,128)(2,1)S(1)}, bf16[8192,512]{1,0:T(8,128)(2,1)S(1)}) custom-call(s32[36]{0:T(128)S(1)} %pad_add_fusion.ctl_ref, ...), custom_call_target="tpu_custom_call", output_to_operand_aliasing={{3}: (3, {}), {4}: (4, {}), {1}: (6, {}), {2}: (7, {})} | custom-call | tf_op jit(solution)/shard_map/forward_step/pallas_call | solution.py:109
  192.6 5.3 %forward_step.30 = (bf16[16,8192]{1,0:T(8,128)(2,1)S(1)}, bf16[11,16,8192]{2,1,0:T(8,128)(2,1)S(1)}, f32[11,16,640]{2,1,0:T(8,128)S(1)}, bf16[8192,512]{1,0:T(8,128)(2,1)S(1)}, bf16[8192,512]{1,0:T(8,128)(2,1)S(1)}) custom-call(s32[36]{0:T(128)S(1)} %pad_add_fusion.ctl_ref, ...), custom_call_target="tpu_custom_call", output_to_operand_aliasing={{3}: (3, {}), {4}: (4, {}), {1}: (6, {}), {2}: (7, {})} | custom-call | tf_op jit(solution)/shard_map/forward_step/pallas_call | solution.py:109
  206.8 5.3 %forward_step.31 = (bf16[16,8192]{1,0:T(8,128)(2,1)S(1)}, bf16[11,16,8192]{2,1,0:T(8,128)(2,1)S(1)}, f32[11,16,640]{2,1,0:T(8,128)S(1)}, bf16[8192,512]{1,0:T(8,128)(2,1)S(1)}, bf16[8192,512]{1,0:T(8,128)(2,1)S(1)}) custom-call(s32[36]{0:T(128)S(1)} %pad_add_fusion.ctl_ref, ...), custom_call_target="tpu_custom_call", output_to_operand_aliasing={{3}: (3, {}), {4}: (4, {}), {1}: (6, {}), {2}: (7, {})} | custom-call | tf_op jit(solution)/shard_map/forward_step/pallas_call | solution.py:109
  220.9 5.3 %forward_step.32 = (bf16[16,8192]{1,0:T(8,128)(2,1)S(1)}, bf16[11,16,8192]{2,1,0:T(8,128)(2,1)S(1)}, f32[11,16,640]{2,1,0:T(8,128)S(1)}, bf16[8192,512]{1,0:T(8,128)(2,1)S(1)}, bf16[8192,512]{1,0:T(8,128)(2,1)S(1)}) custom-call(s32[36]{0:T(128)S(1)} %pad_add_fusion.ctl_ref, ...), custom_call_target="tpu_custom_call", output_to_operand_aliasing={{3}: (3, {}), {4}: (4, {}), {1}: (6, {}), {2}: (7, {})} | custom-call | tf_op jit(solution)/shard_map/forward_step/pallas_call | solution.py:109
  226.3 5.5 %backward_step.25 = (bf16[16,8192]{1,0:T(8,128)(2,1)S(1)}, bf16[11,16,8192]{2,1,0:T(8,128)(2,1)S(1)}, f32[11,16,640]{2,1,0:T(8,128)S(1)}, bf16[11,16,8192]{2,1,0...) custom-call(s32[36]{0:T(128)S(1)} %pad_add_fusion.ctl_ref, ...), custom_call_target="tpu_custom_call", output_to_operand_aliasing={{5}: (3, {}), {6}: (4, {}), {1}: (6, {}), {2}: (7, {}), {3}... | custom-call | tf_op jit(solution)/shard_map/backward_step/pallas_call | solution.py:187
  235.5 6.0 %forward_step.33 = (bf16[16,8192]{1,0:T(8,128)(2,1)}, bf16[11,16,8192]{2,1,0:T(8,128)(2,1)S(1)}, f32[11,16,640]{2,1,0:T(8,128)S(1)}, bf16[8192,512]{1,0:T(8,128)(2,1)S(1)}, bf16[8192,512]{1,0:T(8,128)(2,1)S(1)}) custom-call(s32[36]{0:T(128)S(1)} %pad_add_fusion.ctl_ref, ...), custom_call_target="tpu_custom_call", output_to_operand_aliasing={{3}: (3, {}), {4}: (4, {}), {1}: (6, {}), {2}: (7, {})} | custom-call | tf_op jit(solution)/shard_map/forward_step/pallas_call | solution.py:109
  248.6 5.9 %collective-permute-done.25.came_ref = bf16[16,8192]{1,0:T(8,128)(2,1)S(1)} collective-permute-done((bf16[16,8192]{1,0:T(8,128)(2,1)S(1)}, bf16[16,8192]{1,0:T(8,128)(2,1)S(1)}, u32[]{:S(2)}, u32[]{:S(2)}) %collective-permute-start.25) | collective-permute-done | bytes 262176 | tf_op jit(solution)/shard_map/ppermute | solution.py:253
  333.8 5.8 %backward_step.33 = (bf16[16,8192]{1,0:T(8,128)(2,1)}, bf16[11,16,8192]{2,1,0:T(8,128)(2,1)S(1)}, f32[11,16,640]{2,1,0:T(8,128)S(1)}, bf16[11,16,8192]{2,1,0:T(8...) custom-call(s32[36]{0:T(128)S(1)} %pad_add_fusion.ctl_ref, ...), custom_call_target="tpu_custom_call", output_to_operand_aliasing={{5}: (3, {}), {6}: (4, {}), {1}: (6, {}), {2}: (7, {}), {3}... | custom-call | tf_op jit(solution)/shard_map/backward_step/pallas_call | solution.py:187
  344.6 6.3 %all-to-all-start.2 = ((bf16[8,160,1024]{2,1,0:T(8,128)(2,1)}), bf16[8,160,1024]{2,1,0:T(8,128)(2,1)}, u32[]{:S(2)}, u32[]{:S(2)}) async-start(bf16[8,160,1024]{2,1,0:T(8,128)(2,1)} %bitcast.33), calls=%async_computation.2 | async-start | bytes 5242880 | tf_op jit(solution)/shard_map/all_to_all | solution.py:235
  351.7 18.6 %all-to-all-done.2 = bf16[8,160,1024]{2,1,0:T(8,128)(2,1)} async-done(((bf16[8,160,1024]{2,1,0:T(8,128)(2,1)}), bf16[8,160,1024]{2,1,0:T(8,128)(2,1)}, u32[]{:S(2)}, u32[]{:S(2)}) %all-to-all-start.2) | async-done | bytes 2621472 | tf_op jit(solution)/shard_map/all_to_all | solution.py:235
  382.7 22.4 %all-to-all-done.1 = bf16[8,160,1024]{2,1,0:T(8,128)(2,1)} async-done(((bf16[8,160,1024]{2,1,0:T(8,128)(2,1)}), bf16[8,160,1024]{2,1,0:T(8,128)(2,1)}, u32[]{:S(2)}, u32[]{:S(2)}) %all-to-all-start.1) | async-done | bytes 2621472 | tf_op jit(solution)/shard_map/all_to_all | solution.py:257
  413.5 28.1 %all-to-all-done = bf16[8,160,1024]{2,1,0:T(8,128)(2,1)} async-done(((bf16[8,160,1024]{2,1,0:T(8,128)(2,1)}), bf16[8,160,1024]{2,1,0:T(8,128)(2,1)}, u32[]{:S(2)}, u32[]{:S(2)}) %all-to-all-start) | async-done | bytes 2621472 | tf_op jit(solution)/shard_map/all_to_all | solution.py:235
  447.7 25.6 %collective-permute-start.32 = (bf16[512,1024]{0,1:T(8,128)(2,1)}, bf16[512,1024]{0,1:T(8,128)(2,1)}, u32[]{:S(2)}, u32[]{:S(2)}) collective-permute-start(bf16[512,1024]{0,1:T(8,128)(2,1)} %fusion.1), channel_id=1, source_target_pairs={{0,8},{8,0},{1,9},{9,1},{2,10},{10,2},{3,11},{11,3},{4,12},{12,4},... | collective-permute-start | bytes 3145736 | tf_op jit(solution)/shard_map/ppermute | solution.py:275
  (112 shorter events, 214.7 us)
Async XLA Ops:
  17.6 11.6 %collective-permute-start = (bf16[16,8192]{1,0:T(8,128)(2,1)S(1)}, bf16[16,8192]{1,0:T(8,128)(2,1)S(1)}, u32[]{:S(2)}, u32[]{:S(2)}) collective-permute-start(bf16[16,8192]{1,0:T(8,128)(2,1)S(1)} %get-tuple-element.208), channel_id=1, source_target_pairs={{0,1},{1,2},{2,3},{3,4},{4,5},{5,6},{6,7},{7,0},{8,9},{9,10},{10,1... | collective-permute-start | bytes 786440 | tf_op jit(solution)/shard_map/ppermute | solution.py:247
  34.5 8.8 %collective-permute-start.1 = (bf16[16,8192]{1,0:T(8,128)(2,1)S(1)}, bf16[16,8192]{1,0:T(8,128)(2,1)S(1)}, u32[]{:S(2)}, u32[]{:S(2)}) collective-permute-start(bf16[16,8192]{1,0:T(8,128)(2,1)S(1)} %get-tuple-element.213), channel_id=1, source_target_pairs={{0,1},{1,2},{2,3},{3,4},{4,5},{5,6},{6,7},{7,0},{8,9},{9,10},{10,1... | collective-permute-start | bytes 786440 | tf_op jit(solution)/shard_map/ppermute | solution.py:247
  48.6 7.8 %collective-permute-start.2 = (bf16[16,8192]{1,0:T(8,128)(2,1)S(1)}, bf16[16,8192]{1,0:T(8,128)(2,1)S(1)}, u32[]{:S(2)}, u32[]{:S(2)}) collective-permute-start(bf16[16,8192]{1,0:T(8,128)(2,1)S(1)} %get-tuple-element.218), channel_id=1, source_target_pairs={{0,1},{1,2},{2,3},{3,4},{4,5},{5,6},{6,7},{7,0},{8,9},{9,10},{10,1... | collective-permute-start | bytes 786440 | tf_op jit(solution)/shard_map/ppermute | solution.py:247
  61.8 7.4 %collective-permute-start.3 = (bf16[16,8192]{1,0:T(8,128)(2,1)S(1)}, bf16[16,8192]{1,0:T(8,128)(2,1)S(1)}, u32[]{:S(2)}, u32[]{:S(2)}) collective-permute-start(bf16[16,8192]{1,0:T(8,128)(2,1)S(1)} %get-tuple-element.223), channel_id=1, source_target_pairs={{0,1},{1,2},{2,3},{3,4},{4,5},{5,6},{6,7},{7,0},{8,9},{9,10},{10,1... | collective-permute-start | bytes 786440 | tf_op jit(solution)/shard_map/ppermute | solution.py:247
  112.7 8.9 %collective-permute-start.8 = (bf16[16,8192]{1,0:T(8,128)(2,1)S(1)}, bf16[16,8192]{1,0:T(8,128)(2,1)S(1)}, u32[]{:S(2)}, u32[]{:S(2)}) collective-permute-start(bf16[16,8192]{1,0:T(8,128)(2,1)S(1)} %get-tuple-element.248), channel_id=1, source_target_pairs={{0,1},{1,2},{2,3},{3,4},{4,5},{5,6},{6,7},{7,0},{8,9},{9,10},{10,1... | collective-permute-start | bytes 786440 | tf_op jit(solution)/shard_map/ppermute | solution.py:247
  117.9 9.0 %collective-permute-start.7 = (bf16[16,8192]{1,0:T(8,128)(2,1)S(1)}, bf16[16,8192]{1,0:T(8,128)(2,1)S(1)}, u32[]{:S(2)}, u32[]{:S(2)}) collective-permute-start(bf16[16,8192]{1,0:T(8,128)(2,1)S(1)} %get-tuple-element.247), channel_id=1, source_target_pairs={{1,0},{2,1},{3,2},{4,3},{5,4},{6,5},{7,6},{0,7},{9,8},{10,9},{11,1... | collective-permute-start | bytes 786440 | tf_op jit(solution)/shard_map/ppermute | solution.py:253
  126.9 8.8 %collective-permute-start.10 = (bf16[16,8192]{1,0:T(8,128)(2,1)S(1)}, bf16[16,8192]{1,0:T(8,128)(2,1)S(1)}, u32[]{:S(2)}, u32[]{:S(2)}) collective-permute-start(bf16[16,8192]{1,0:T(8,128)(2,1)S(1)} %get-tuple-element.260), channel_id=1, source_target_pairs={{0,1},{1,2},{2,3},{3,4},{4,5},{5,6},{6,7},{7,0},{8,9},{9,10},{10,1... | collective-permute-start | bytes 786440 | tf_op jit(solution)/shard_map/ppermute | solution.py:247
  132.1 9.3 %collective-permute-start.9 = (bf16[16,8192]{1,0:T(8,128)(2,1)S(1)}, bf16[16,8192]{1,0:T(8,128)(2,1)S(1)}, u32[]{:S(2)}, u32[]{:S(2)}) collective-permute-start(bf16[16,8192]{1,0:T(8,128)(2,1)S(1)} %get-tuple-element.259), channel_id=1, source_target_pairs={{1,0},{2,1},{3,2},{4,3},{5,4},{6,5},{7,6},{0,7},{9,8},{10,9},{11,1... | collective-permute-start | bytes 786440 | tf_op jit(solution)/shard_map/ppermute | solution.py:253
  141.1 9.0 %collective-permute-start.12 = (bf16[16,8192]{1,0:T(8,128)(2,1)S(1)}, bf16[16,8192]{1,0:T(8,128)(2,1)S(1)}, u32[]{:S(2)}, u32[]{:S(2)}) collective-permute-start(bf16[16,8192]{1,0:T(8,128)(2,1)S(1)} %get-tuple-element.272), channel_id=1, source_target_pairs={{0,1},{1,2},{2,3},{3,4},{4,5},{5,6},{6,7},{7,0},{8,9},{9,10},{10,1... | collective-permute-start | bytes 786440 | tf_op jit(solution)/shard_map/ppermute | solution.py:247
  146.5 9.0 %collective-permute-start.11 = (bf16[16,8192]{1,0:T(8,128)(2,1)S(1)}, bf16[16,8192]{1,0:T(8,128)(2,1)S(1)}, u32[]{:S(2)}, u32[]{:S(2)}) collective-permute-start(bf16[16,8192]{1,0:T(8,128)(2,1)S(1)} %get-tuple-element.271), channel_id=1, source_target_pairs={{1,0},{2,1},{3,2},{4,3},{5,4},{6,5},{7,6},{0,7},{9,8},{10,9},{11,1... | collective-permute-start | bytes 786440 | tf_op jit(solution)/shard_map/ppermute | solution.py:253
  155.4 8.8 %collective-permute-start.14 = (bf16[16,8192]{1,0:T(8,128)(2,1)S(1)}, bf16[16,8192]{1,0:T(8,128)(2,1)S(1)}, u32[]{:S(2)}, u32[]{:S(2)}) collective-permute-start(bf16[16,8192]{1,0:T(8,128)(2,1)S(1)} %get-tuple-element.284), channel_id=1, source_target_pairs={{0,1},{1,2},{2,3},{3,4},{4,5},{5,6},{6,7},{7,0},{8,9},{9,10},{10,1... | collective-permute-start | bytes 786440 | tf_op jit(solution)/shard_map/ppermute | solution.py:247
  160.7 9.0 %collective-permute-start.13 = (bf16[16,8192]{1,0:T(8,128)(2,1)S(1)}, bf16[16,8192]{1,0:T(8,128)(2,1)S(1)}, u32[]{:S(2)}, u32[]{:S(2)}) collective-permute-start(bf16[16,8192]{1,0:T(8,128)(2,1)S(1)} %get-tuple-element.283), channel_id=1, source_target_pairs={{1,0},{2,1},{3,2},{4,3},{5,4},{6,5},{7,6},{0,7},{9,8},{10,9},{11,1... | collective-permute-start | bytes 786440 | tf_op jit(solution)/shard_map/ppermute | solution.py:253
  169.6 8.8 %collective-permute-start.16 = (bf16[16,8192]{1,0:T(8,128)(2,1)S(1)}, bf16[16,8192]{1,0:T(8,128)(2,1)S(1)}, u32[]{:S(2)}, u32[]{:S(2)}) collective-permute-start(bf16[16,8192]{1,0:T(8,128)(2,1)S(1)} %get-tuple-element.296), channel_id=1, source_target_pairs={{0,1},{1,2},{2,3},{3,4},{4,5},{5,6},{6,7},{7,0},{8,9},{9,10},{10,1... | collective-permute-start | bytes 786440 | tf_op jit(solution)/shard_map/ppermute | solution.py:247
  174.8 9.0 %collective-permute-start.15 = (bf16[16,8192]{1,0:T(8,128)(2,1)S(1)}, bf16[16,8192]{1,0:T(8,128)(2,1)S(1)}, u32[]{:S(2)}, u32[]{:S(2)}) collective-permute-start(bf16[16,8192]{1,0:T(8,128)(2,1)S(1)} %get-tuple-element.295), channel_id=1, source_target_pairs={{1,0},{2,1},{3,2},{4,3},{5,4},{6,5},{7,6},{0,7},{9,8},{10,9},{11,1... | collective-permute-start | bytes 786440 | tf_op jit(solution)/shard_map/ppermute | solution.py:253
  183.8 8.8 %collective-permute-start.18 = (bf16[16,8192]{1,0:T(8,128)(2,1)S(1)}, bf16[16,8192]{1,0:T(8,128)(2,1)S(1)}, u32[]{:S(2)}, u32[]{:S(2)}) collective-permute-start(bf16[16,8192]{1,0:T(8,128)(2,1)S(1)} %get-tuple-element.308), channel_id=1, source_target_pairs={{0,1},{1,2},{2,3},{3,4},{4,5},{5,6},{6,7},{7,0},{8,9},{9,10},{10,1... | collective-permute-start | bytes 786440 | tf_op jit(solution)/shard_map/ppermute | solution.py:247
  189.0 9.0 %collective-permute-start.17 = (bf16[16,8192]{1,0:T(8,128)(2,1)S(1)}, bf16[16,8192]{1,0:T(8,128)(2,1)S(1)}, u32[]{:S(2)}, u32[]{:S(2)}) collective-permute-start(bf16[16,8192]{1,0:T(8,128)(2,1)S(1)} %get-tuple-element.307), channel_id=1, source_target_pairs={{1,0},{2,1},{3,2},{4,3},{5,4},{6,5},{7,6},{0,7},{9,8},{10,9},{11,1... | collective-permute-start | bytes 786440 | tf_op jit(solution)/shard_map/ppermute | solution.py:253
  197.9 8.8 %collective-permute-start.20 = (bf16[16,8192]{1,0:T(8,128)(2,1)S(1)}, bf16[16,8192]{1,0:T(8,128)(2,1)S(1)}, u32[]{:S(2)}, u32[]{:S(2)}) collective-permute-start(bf16[16,8192]{1,0:T(8,128)(2,1)S(1)} %get-tuple-element.320), channel_id=1, source_target_pairs={{0,1},{1,2},{2,3},{3,4},{4,5},{5,6},{6,7},{7,0},{8,9},{9,10},{10,1... | collective-permute-start | bytes 786440 | tf_op jit(solution)/shard_map/ppermute | solution.py:247
  203.1 9.0 %collective-permute-start.19 = (bf16[16,8192]{1,0:T(8,128)(2,1)S(1)}, bf16[16,8192]{1,0:T(8,128)(2,1)S(1)}, u32[]{:S(2)}, u32[]{:S(2)}) collective-permute-start(bf16[16,8192]{1,0:T(8,128)(2,1)S(1)} %get-tuple-element.319), channel_id=1, source_target_pairs={{1,0},{2,1},{3,2},{4,3},{5,4},{6,5},{7,6},{0,7},{9,8},{10,9},{11,1... | collective-permute-start | bytes 786440 | tf_op jit(solution)/shard_map/ppermute | solution.py:253
  212.1 8.8 %collective-permute-start.22 = (bf16[16,8192]{1,0:T(8,128)(2,1)S(1)}, bf16[16,8192]{1,0:T(8,128)(2,1)S(1)}, u32[]{:S(2)}, u32[]{:S(2)}) collective-permute-start(bf16[16,8192]{1,0:T(8,128)(2,1)S(1)} %get-tuple-element.332), channel_id=1, source_target_pairs={{0,1},{1,2},{2,3},{3,4},{4,5},{5,6},{6,7},{7,0},{8,9},{9,10},{10,1... | collective-permute-start | bytes 786440 | tf_op jit(solution)/shard_map/ppermute | solution.py:247
  217.3 9.0 %collective-permute-start.21 = (bf16[16,8192]{1,0:T(8,128)(2,1)S(1)}, bf16[16,8192]{1,0:T(8,128)(2,1)S(1)}, u32[]{:S(2)}, u32[]{:S(2)}) collective-permute-start(bf16[16,8192]{1,0:T(8,128)(2,1)S(1)} %get-tuple-element.331), channel_id=1, source_target_pairs={{1,0},{2,1},{3,2},{4,3},{5,4},{6,5},{7,6},{0,7},{9,8},{10,9},{11,1... | collective-permute-start | bytes 786440 | tf_op jit(solution)/shard_map/ppermute | solution.py:253
  226.2 9.2 %collective-permute-start.24 = (bf16[16,8192]{1,0:T(8,128)(2,1)S(1)}, bf16[16,8192]{1,0:T(8,128)(2,1)S(1)}, u32[]{:S(2)}, u32[]{:S(2)}) collective-permute-start(bf16[16,8192]{1,0:T(8,128)(2,1)S(1)} %get-tuple-element.344), channel_id=1, source_target_pairs={{0,1},{1,2},{2,3},{3,4},{4,5},{5,6},{6,7},{7,0},{8,9},{9,10},{10,1... | collective-permute-start | bytes 786440 | tf_op jit(solution)/shard_map/ppermute | solution.py:247
  231.8 9.6 %collective-permute-start.23 = (bf16[16,8192]{1,0:T(8,128)(2,1)S(1)}, bf16[16,8192]{1,0:T(8,128)(2,1)S(1)}, u32[]{:S(2)}, u32[]{:S(2)}) collective-permute-start(bf16[16,8192]{1,0:T(8,128)(2,1)S(1)} %get-tuple-element.343), channel_id=1, source_target_pairs={{1,0},{2,1},{3,2},{4,3},{5,4},{6,5},{7,6},{0,7},{9,8},{10,9},{11,1... | collective-permute-start | bytes 786440 | tf_op jit(solution)/shard_map/ppermute | solution.py:253
  246.6 7.9 %collective-permute-start.25 = (bf16[16,8192]{1,0:T(8,128)(2,1)S(1)}, bf16[16,8192]{1,0:T(8,128)(2,1)S(1)}, u32[]{:S(2)}, u32[]{:S(2)}) collective-permute-start(bf16[16,8192]{1,0:T(8,128)(2,1)S(1)} %get-tuple-element.355), channel_id=1, source_target_pairs={{1,0},{2,1},{3,2},{4,3},{5,4},{6,5},{7,6},{0,7},{9,8},{10,9},{11,1... | collective-permute-start | bytes 786440 | tf_op jit(solution)/shard_map/ppermute | solution.py:253
  259.6 9.4 %collective-permute-start.26 = (bf16[16,8192]{1,0:T(8,128)(2,1)S(1)}, bf16[16,8192]{1,0:T(8,128)(2,1)S(1)}, u32[]{:S(2)}, u32[]{:S(2)}) collective-permute-start(bf16[16,8192]{1,0:T(8,128)(2,1)S(1)} %get-tuple-element.362), channel_id=1, source_target_pairs={{1,0},{2,1},{3,2},{4,3},{5,4},{6,5},{7,6},{0,7},{9,8},{10,9},{11,1... | collective-permute-start | bytes 786440 | tf_op jit(solution)/shard_map/ppermute | solution.py:253
  274.1 8.7 %collective-permute-start.27 = (bf16[16,8192]{1,0:T(8,128)(2,1)S(1)}, bf16[16,8192]{1,0:T(8,128)(2,1)S(1)}, u32[]{:S(2)}, u32[]{:S(2)}) collective-permute-start(bf16[16,8192]{1,0:T(8,128)(2,1)S(1)} %get-tuple-element.369), channel_id=1, source_target_pairs={{1,0},{2,1},{3,2},{4,3},{5,4},{6,5},{7,6},{0,7},{9,8},{10,9},{11,1... | collective-permute-start | bytes 786440 | tf_op jit(solution)/shard_map/ppermute | solution.py:253
  288.0 7.7 %collective-permute-start.28 = (bf16[16,8192]{1,0:T(8,128)(2,1)S(1)}, bf16[16,8192]{1,0:T(8,128)(2,1)S(1)}, u32[]{:S(2)}, u32[]{:S(2)}) collective-permute-start(bf16[16,8192]{1,0:T(8,128)(2,1)S(1)} %get-tuple-element.376), channel_id=1, source_target_pairs={{1,0},{2,1},{3,2},{4,3},{5,4},{6,5},{7,6},{0,7},{9,8},{10,9},{11,1... | collective-permute-start | bytes 786440 | tf_op jit(solution)/shard_map/ppermute | solution.py:253
  300.8 7.8 %collective-permute-start.29 = (bf16[16,8192]{1,0:T(8,128)(2,1)S(1)}, bf16[16,8192]{1,0:T(8,128)(2,1)S(1)}, u32[]{:S(2)}, u32[]{:S(2)}) collective-permute-start(bf16[16,8192]{1,0:T(8,128)(2,1)S(1)} %get-tuple-element.383), channel_id=1, source_target_pairs={{1,0},{2,1},{3,2},{4,3},{5,4},{6,5},{7,6},{0,7},{9,8},{10,9},{11,1... | collective-permute-start | bytes 786440 | tf_op jit(solution)/shard_map/ppermute | solution.py:253
  326.2 7.6 %collective-permute-start.31 = (bf16[16,8192]{1,0:T(8,128)(2,1)S(1)}, bf16[16,8192]{1,0:T(8,128)(2,1)S(1)}, u32[]{:S(2)}, u32[]{:S(2)}) collective-permute-start(bf16[16,8192]{1,0:T(8,128)(2,1)S(1)} %get-tuple-element.397), channel_id=1, source_target_pairs={{1,0},{2,1},{3,2},{4,3},{5,4},{6,5},{7,6},{0,7},{9,8},{10,9},{11,1... | collective-permute-start | bytes 786440 | tf_op jit(solution)/shard_map/ppermute | solution.py:253
  344.6 25.7 %all-to-all-start.2 = ((bf16[8,160,1024]{2,1,0:T(8,128)(2,1)}), bf16[8,160,1024]{2,1,0:T(8,128)(2,1)}, u32[]{:S(2)}, u32[]{:S(2)}) async-start(bf16[8,160,1024]{2,1,0:T(8,128)(2,1)} %bitcast.33), calls=%async_computation.2 | async-start | bytes 5242880 | tf_op jit(solution)/shard_map/all_to_all | solution.py:235
  373.2 32.0 %all-to-all-start.1 = ((bf16[8,160,1024]{2,1,0:T(8,128)(2,1)}), bf16[8,160,1024]{2,1,0:T(8,128)(2,1)}, u32[]{:S(2)}, u32[]{:S(2)}) async-start(bf16[8,160,1024]{2,1,0:T(8,128)(2,1)} %broadcast_in_dim.20), calls=%async_computation.1 | async-start | bytes 5242880 | tf_op jit(solution)/shard_map/all_to_all | solution.py:257
  405.2 36.4 %all-to-all-start = ((bf16[8,160,1024]{2,1,0:T(8,128)(2,1)}), bf16[8,160,1024]{2,1,0:T(8,128)(2,1)}, u32[]{:S(2)}, u32[]{:S(2)}) async-start(bf16[8,160,1024]{2,1,0:T(8,128)(2,1)} %bitcast.30), calls=%async_computation | async-start | bytes 5242880 | tf_op jit(solution)/shard_map/all_to_all | solution.py:235
  447.7 28.2 %collective-permute-start.32 = (bf16[512,1024]{0,1:T(8,128)(2,1)}, bf16[512,1024]{0,1:T(8,128)(2,1)}, u32[]{:S(2)}, u32[]{:S(2)}) collective-permute-start(bf16[512,1024]{0,1:T(8,128)(2,1)} %fusion.1), channel_id=1, source_target_pairs={{0,8},{8,0},{1,9},{9,1},{2,10},{10,2},{3,11},{11,3},{4,12},{12,4},... | collective-permute-start | bytes 3145736 | tf_op jit(solution)/shard_map/ppermute | solution.py:275
  (11 other events, 63.7 us)
where the time goes:
time: 491 us; the launch traced here: 482 us
  Pallas kernels  180 us (37%)
  waiting for transfers between devices  153 us (31%)
  starting transfers between devices  105 us (21%)
  local copies, waits for them, and re-layouts  29.7 us (6%)
  matrix products  7.31 us (1%)
    pallas_call x17, Pallas kernels, forward_step(): pl.pallas_call(functools.partial(forward_body, tick, micro), out_shape=(j...  92.2 us
    pallas_call x17, Pallas kernels, backward_step(): pl.pallas_call(functools.partial(backward_body, tick, micro, last), out_s...  87.9 us
    ppermute x16, starting transfers between devices, local(): arriving = lax.ppermute(made, 'section', back)  60.3 us
    ppermute x16, waiting for transfers between devices, local(): came = lax.ppermute(made, 'section', onward)  54.8 us
    all_to_all x2, waiting for transfers between devices, spread(): return lax.all_to_all(tiles, CHIPS, split_axis=0, concat_axis=0, tiled=True)  46.7 us
    ppermute x16, waiting for transfers between devices, local(): arriving = lax.ppermute(made, 'section', back)  28.8 us
    ppermute x1, starting transfers between devices, local(): lax.ppermute(theirs, CORE, [(0, 1), (1, 0)]).astype(jnp.float32)  25.6 us
    all_to_all x1, waiting for transfers between devices, local(): lax.all_to_all(jnp.broadcast_to(pair, (chips, tokens, 2 * hidden)), CHIPS...  22.4 us
  transfers between devices with their start and end apart: 36, of which 18 were waited for; matrix products, arithmetic and copies ran while one was open for 2% of the time, Pallas kernels for 20%

commit v1 on v0

v1 whole, which is shorter than its diff:
```python
import functools

import jax
import jax.numpy as jnp
from jax import lax
from jax.experimental import pallas as pl
from jax.experimental.pallas import tpu as pltpu
from jax.sharding import Mesh
from jax.sharding import PartitionSpec as P

ROWS = 16
EARLY = 7
WAIT = 4
UNROLL = 8
SCOPED = 6 << 20
DP = ("dp_0", "dp_1", "dp_2")
CHIPS = ("dp_0", "dp_1")
CORE = "dp_2"
EPSILON = 1e-05

VMEM = pl.BlockSpec(memory_space=pltpu.VMEM)
SMEM = pl.BlockSpec(memory_space=pltpu.SMEM)
HBM = pl.BlockSpec(memory_space=pltpu.HBM)


def bring_in(low, micro, mine, came_ref, source_ref, rows_ref, sem):
    def fetch():
        copy = pltpu.make_async_copy(source_ref.at[pl.ds(low * ROWS, ROWS), :], rows_ref, sem)
        copy.start()
        copy.wait()

    if came_ref is None:
        fetch()
    elif not 0 <= low < micro:
        rows_ref[...] = came_ref[...]
    else:
        pl.when(mine)(fetch)

        @pl.when(jnp.logical_not(mine))
        def _():
            rows_ref[...] = came_ref[...]


def turned(k, ctl_ref, pieces):
    away = k - ctl_ref[ctl_ref.shape[0] - 3]
    return jnp.where(away < 0, away + pieces, away)


def column_cut(k, size):
    return pl.ds(pl.multiple_of(k * size, size), size)


def forward_body(tick, micro, *refs):
    starting = tick == 0
    ctl_ref, source_ref, w_in_far, w_out_far, gain_ref, *refs = refs
    came_ref = None if starting else refs[0]
    (out_ref, rows_all, pre_all, w_in_ref, w_out_ref, rows_ref, source_sem, load_sem) = refs[-8:]
    width, hidden = w_in_ref.shape
    pieces, _, _, size = rows_all.shape
    slot = ctl_ref[tick]

    def load(which, k):
        far, near = ((w_in_far, w_in_ref), (w_out_far, w_out_ref))[which]
        cut = column_cut(k, size)
        return pltpu.make_async_copy(far.at[cut, :], near.at[cut, :], load_sem.at[which, k])

    if starting:
        for which in range(2):
            for k in range(pieces):
                load(which, k).start()
    mine = ctl_ref[ctl_ref.shape[0] - 2] == 1
    bring_in(tick, micro, mine, came_ref, source_ref, rows_ref, source_sem)

    def project(k, carry):
        pre, total = carry
        if starting:
            load(0, k).wait()
        cut = column_cut(k, size)
        rows = rows_ref[:, cut]
        rows_all[turned(k, ctl_ref, pieces), slot] = rows
        rows = rows.astype(jnp.float32)
        pre = pre + jnp.dot(
            (rows * gain_ref[:, cut]).astype(jnp.bfloat16), w_in_ref[cut, :], preferred_element_type=jnp.float32
        )
        return pre, total + jnp.sum(rows * rows, axis=1, keepdims=True)

    zeros = jnp.zeros((ROWS, hidden), jnp.float32), jnp.zeros((ROWS, 1), jnp.float32)
    pre, total = lax.fori_loop(0, pieces, project, zeros, unroll=UNROLL)
    row_scale = lax.rsqrt(total / width + EPSILON)
    pre = pre * row_scale
    pre_all[slot, :, :hidden] = pre
    pre_all[slot, :, hidden:] = jnp.broadcast_to(row_scale, (ROWS, 128))
    act = (pre * jax.nn.sigmoid(pre)).astype(jnp.bfloat16)

    def expand(k, carry):
        if starting:
            load(1, k).wait()
        cut = column_cut(k, size)
        branch = lax.dot_general(
            act, w_out_ref[cut, :], (((1,), (1,)), ((), ())), preferred_element_type=jnp.float32
        )
        out_ref[:, cut] = (rows_ref[:, cut].astype(jnp.float32) + branch).astype(jnp.bfloat16)
        return carry

    lax.fori_loop(0, pieces, expand, 0, unroll=UNROLL)


def forward_step(tick, micro, pieces, ctl, source, w_in, w_out, gain, came, stores):
    width, hidden = w_in.shape
    starting = tick == 0
    weight = HBM if starting else VMEM
    return pl.pallas_call(
        functools.partial(forward_body, tick, micro),
        out_shape=(
            jax.ShapeDtypeStruct((ROWS, width), jnp.bfloat16),
            pltpu.VMEM((pieces, micro + 1, ROWS, width // pieces), jnp.bfloat16),
            pltpu.VMEM((micro + 1, ROWS, hidden + 128), jnp.float32),
            pltpu.VMEM(w_in.shape, jnp.bfloat16),
            pltpu.VMEM(w_out.shape, jnp.bfloat16),
        ),
        in_specs=[SMEM, HBM, weight, weight, VMEM] + [VMEM] * (0 if starting else 3),
        out_specs=(VMEM,) * 5,
        scratch_shapes=[
            pltpu.VMEM((ROWS, width), jnp.bfloat16),
            pltpu.SemaphoreType.DMA,
            pltpu.SemaphoreType.DMA((2, pieces)),
        ],
        input_output_aliases={} if starting else {2: 3, 3: 4, 6: 1, 7: 2},
        compiler_params=pltpu.CompilerParams(vmem_limit_bytes=SCOPED),
        name="forward_step",
    )(ctl, source, w_in, w_out, gain, *(() if starting else (came, *stores)))


def backward_body(tick, micro, last, *refs):
    starting = tick == last
    ctl_ref, source_ref, w_in_in, w_out_in, gain_ref, rows_in, pre_in, *refs = refs
    came_ref = None if starting else refs[0]
    (out_ref, rows_all, pre_all, both_all, w_in_ref, w_out_ref, up_ref, sem) = refs[-8:]
    width, hidden = w_in_ref.shape
    pieces, _, _, size = rows_all.shape
    slot = ctl_ref[micro + tick]
    mine = ctl_ref[ctl_ref.shape[0] - 1] == 1
    bring_in(tick - last, micro, mine, came_ref, source_ref, up_ref, sem)

    def project(k, total):
        cut = column_cut(k, size)
        up = up_ref[:, cut]
        both_all[turned(k, ctl_ref, pieces), slot, :, :size] = up
        return total + jnp.dot(up, w_out_ref[cut, :], preferred_element_type=jnp.float32)

    grad_act = lax.fori_loop(0, pieces, project, jnp.zeros((ROWS, hidden), jnp.float32), unroll=UNROLL)
    pre = pre_all[slot, :, :hidden]
    row_scale = pre_all[slot, :, hidden : hidden + 1]
    sig = jax.nn.sigmoid(pre)
    grad_pre = grad_act * sig * (1.0 + pre * (1.0 - sig))
    scaled = (grad_pre * row_scale).astype(jnp.bfloat16)
    act = (pre * sig).astype(jnp.bfloat16)
    for k in range(pieces):
        both_all[k, slot, :, size : size + hidden] = scaled
        both_all[k, slot, :, size + hidden :] = act
    pull = jnp.sum(scaled.astype(jnp.float32) * pre, axis=1, keepdims=True) * row_scale / width

    def expand(k, carry):
        cut = column_cut(k, size)
        grad_norm = lax.dot_general(
            scaled, w_in_ref[cut, :], (((1,), (1,)), ((), ())), preferred_element_type=jnp.float32
        )
        out_ref[:, cut] = (
            up_ref[:, cut].astype(jnp.float32)
            + grad_norm * gain_ref[:, cut]
            - rows_all[turned(k, ctl_ref, pieces), slot].astype(jnp.float32) * pull
        ).astype(jnp.bfloat16)
        return carry

    lax.fori_loop(0, pieces, expand, 0, unroll=UNROLL)


def backward_step(tick, micro, last, pieces, ctl, source, w_in, w_out, gain, stores, came, kept):
    width, hidden = w_in.shape
    starting = tick == last
    size = width // pieces
    return pl.pallas_call(
        functools.partial(backward_body, tick, micro, last),
        out_shape=(
            jax.ShapeDtypeStruct((ROWS, width), jnp.bfloat16),
            pltpu.VMEM((pieces, micro + 1, ROWS, size), jnp.bfloat16),
            pltpu.VMEM((micro + 1, ROWS, hidden + 128), jnp.float32),
            pltpu.VMEM((pieces, micro + 1, ROWS, size + 2 * hidden), jnp.bfloat16),
            pltpu.VMEM(w_in.shape, jnp.bfloat16),
            pltpu.VMEM(w_out.shape, jnp.bfloat16),
        ),
        in_specs=[SMEM, HBM] + [VMEM] * (5 if starting else 7),
        out_specs=(VMEM,) * 6,
        scratch_shapes=[pltpu.VMEM((ROWS, width), jnp.bfloat16), pltpu.SemaphoreType.DMA],
        input_output_aliases={2: 4, 3: 5, 5: 1, 6: 2, **({} if starting else {8: 3})},
        compiler_params=pltpu.CompilerParams(vmem_limit_bytes=SCOPED),
        name="backward_step",
    )(ctl, source, w_in, w_out, gain, *stores, *(() if starting else (came, kept)))


def gradient_body(counts, span, ctl_ref, *refs):
    parts, adding, splitting = counts
    sources, refs = refs[: 2 * parts], refs[2 * parts :]
    rows_buf, both_buf, sems = refs[-3:]
    copies = []
    each = span[1] - span[0]
    for k, source in enumerate(sources):
        buf = rows_buf if k < parts else both_buf
        source = source.at[pl.ds(span[0], each), :] if k < parts else source
        at = pl.ds(k % parts * each, each)
        copies.append(pltpu.make_async_copy(source, buf.at[at, :], sems.at[k]))
    for copy in copies:
        copy.start()
    for copy in copies:
        copy.wait()
    size = rows_buf.shape[1]
    hidden = (both_buf.shape[1] - size) // 2
    core = ctl_ref[ctl_ref.shape[0] - 4]

    def product(left, right):
        return lax.dot_general(left, right, (((0,), (0,)), ((), ())), preferred_element_type=jnp.float32)

    half = size // 2
    for which in range(2):
        low = pl.multiple_of((core if which == 0 else 1 - core) * half, half) if splitting else which * half
        rows = rows_buf[:, pl.ds(low, half)]
        ups = both_buf[:, pl.ds(low, half)]
        for side, value in enumerate(
            (product(rows, both_buf[:, size : size + hidden]), product(ups, both_buf[:, size + hidden :]))
        ):
            at = slice(side * hidden, (side + 1) * hidden)
            if adding:
                value = value + refs[0][pl.ds(low, half), at]
            if splitting:
                out_ref = refs[adding + which]
                out_ref[:, at] = value.astype(out_ref.dtype)
            else:
                refs[adding][pl.ds(low, half), at] = value


def gradient_step(ctl, rows, both, span, before, splitting):
    size = rows[0].shape[1]
    each = span[1] - span[0]
    pair = both[0].shape[1] - size
    tokens = each * len(rows)
    if splitting:
        out_shape = (
            jax.ShapeDtypeStruct((size // 2, pair), jnp.float32),
            jax.ShapeDtypeStruct((size // 2, pair), jnp.bfloat16),
        )
    else:
        out_shape = (jax.ShapeDtypeStruct((size, pair), jnp.float32),)
    adding = 0 if before is None else 1
    return pl.pallas_call(
        functools.partial(gradient_body, (len(rows), adding, splitting), span),
        out_shape=out_shape,
        in_specs=[SMEM] + [pl.BlockSpec(memory_space=pl.ANY)] * (2 * len(rows)) + [VMEM] * adding,
        out_specs=(VMEM,) * len(out_shape),
        scratch_shapes=[
            pltpu.VMEM((tokens, size), jnp.bfloat16),
            pltpu.VMEM((tokens, size + pair), jnp.bfloat16),
            pltpu.SemaphoreType.DMA((2 * len(rows),)),
        ],
        compiler_params=pltpu.CompilerParams(vmem_limit_bytes=26 << 20),
        name="gradient_step",
    )(ctl, *rows, *both, *(() if before is None else (before,)))


def finish_body(mine_ref, came_ref, w_ref, gain_ref, in_ref, out_ref, sum_ref):
    hidden = in_ref.shape[1]
    total = mine_ref[...] + came_ref[...].astype(jnp.float32)
    plain = total[:, :hidden]
    in_ref[...] = plain * gain_ref[:, :1]
    out_ref[...] = total[:, hidden:]
    sum_ref[...] = jnp.sum(plain * w_ref[...].astype(jnp.float32), axis=1, keepdims=True)


def local(inputs, cotangent, weight_in, weight_out, norm_gains):
    gain = norm_gains
    tokens, width = inputs.shape
    hidden = weight_in.shape[2]
    micro = tokens // ROWS
    sections = lax.axis_size("section")
    last = sections - 1
    pos = lax.axis_index("section")
    chips = lax.axis_size(CHIPS)
    half = width // (chips * lax.axis_size(CORE))
    onward = [(i, (i + 1) % sections) for i in range(sections)]
    back = [((i + 1) % sections, i) for i in range(sections)]
    ticks = jnp.arange(micro + last)
    which = jnp.concatenate([ticks - pos, ticks - last + pos])
    slots = jnp.where((which >= 0) & (which < micro), which, micro)
    own = jnp.stack([lax.axis_index(CORE), lax.axis_index(CHIPS), pos == 0, pos == last])
    ctl = jnp.concatenate([slots, own]).astype(jnp.int32)
    low = lax.axis_index(DP) * half
    gain_cut = jnp.broadcast_to(lax.dynamic_slice_in_dim(gain[0], low, half, 0)[:, None], (half, 128))
    w_cut = lax.dynamic_slice_in_dim(weight_in[0], low, half, 0)
    ctl, gain_cut, w_cut, inputs, cotangent, w_in_near, w_out_near = lax.optimization_barrier(
        (ctl, gain_cut, w_cut, inputs, cotangent, weight_in[0], weight_out[0])
    )
    inputs, cotangent, w_in_near, w_out_near = (
        pltpu.with_memory_space_constraint(array, pltpu.HBM)
        for array in (inputs, cotangent, w_in_near, w_out_near)
    )

    def hand_round(tiles):
        tiles = tiles.reshape(chips, -1, tiles.shape[-1])
        return [tiles[0]] + [
            lax.ppermute(tiles[d], CHIPS, [(i, (i + d) % chips) for i in range(chips)]) for d in range(1, chips)
        ]

    def by_now(array, others):
        array, *others = lax.optimization_barrier((array, *others))
        return array, others

    stores = kept = came = arriving = None
    rows_all = both_early = None
    for tick in range(micro + 2 * last):
        if tick < micro + last:
            made, *stores, w_in_near, w_out_near = forward_step(
                tick, micro, chips, ctl, inputs, w_in_near, w_out_near, gain, came, stores
            )
            came = lax.ppermute(made, "section", onward)
        if tick == micro - 1 + last:
            rows_all = hand_round(stores[0][:, :micro])
        if tick == micro - 1 + last + WAIT:
            arriving, rows_all = by_now(arriving, rows_all)
        if tick >= last:
            made, *stores, kept, w_in_near, w_out_near = backward_step(
                tick, micro, last, chips, ctl, cotangent, w_in_near, w_out_near, gain, stores, arriving, kept
            )
            if tick < micro + 2 * last - 1:
                arriving = lax.ppermute(made, "section", back)
        if tick == EARLY - 1 + 2 * last:
            both_early = hand_round(kept[:, :EARLY])
    cut = EARLY * ROWS
    (before,) = gradient_step(ctl, rows_all, both_early, (0, cut), None, False)
    both_late = hand_round(kept[:, EARLY:micro])
    mine, theirs = gradient_step(ctl, rows_all, both_late, (cut, tokens), before, True)
    theirs = lax.ppermute(theirs, CORE, [(0, 1), (1, 0)])
    in_grad, out_grad, gain_grad = pl.pallas_call(
        finish_body,
        out_shape=(
            jax.ShapeDtypeStruct((half, hidden), jnp.float32),
            jax.ShapeDtypeStruct((half, hidden), jnp.float32),
            jax.ShapeDtypeStruct((half, 1), jnp.float32),
        ),
        in_specs=[VMEM] * 4,
        out_specs=(VMEM,) * 3,
        name="finish",
    )(mine, theirs, w_cut, gain_cut)
    return (in_grad[None], out_grad[None], gain_grad.reshape(1, half))


def solution(mesh):
    finer = Mesh(
        mesh.devices.reshape(2, 4, 2, mesh.shape["section"]), ("dp_0", "dp_1", "dp_2", "section")
    )
    in_specs = (
        P(DP, None),
        P(DP, None),
        P("section", None, None),
        P("section", None, None),
        P("section", None),
    )
    out_specs = (P("section", DP, None), P("section", DP, None), P("section", DP))
    return jax.shard_map(local, mesh=finer, in_specs=in_specs, out_specs=out_specs, check_vma=False)
```

time: 491 us -> 441 us (0.90)
  waiting for transfers between devices: 153 us -> 106 us
  starting transfers between devices: 105 us -> 142 us
  local copies, waits for them, and re-layouts: 29.7 us -> 7.32 us
  matrix products: 7.31 us -> 0 us
  Pallas kernels: 180 us -> 174 us
    all_to_all x3 -> x0, waiting for transfers between devices: 69.2 us -> none  [the longest x2 46.7 us: spread(): return lax.all_to_all(tiles, CHIPS, split_axis=0, concat_axis=0, tiled=True)]
    ppermute x1 -> x22, starting transfers between devices: 25.6 us -> 78.8 us  [the longest x21 49 us: hand_round(): lax.ppermute(tiles[d], CHIPS, [(i, (i + d) % chips) for i in range(chips)])]
    ppermute x1 -> x22, waiting for transfers between devices: 0.64 us -> 34.2 us  [the longest x21 31.9 us: hand_round(): lax.ppermute(tiles[d], CHIPS, [(i, (i + d) % chips) for i in range(chips)])]
    pallas_call x17, Pallas kernels: 87.9 us -> 70.5 us  [backward_step(): pl.pallas_call(functools.partial(backward_body, tick, micro, last), out_s...]
    pallas_call x0 -> x3, Pallas kernels: none -> 16.5 us  [the longest x2 12.8 us: gradient_step(): pl.pallas_call(functools.partial(gradient_body, (len(rows), adding, split...]
    all_to_all x3 -> x0, starting transfers between devices: 15.6 us -> none  [the longest x2 11 us: spread(): return lax.all_to_all(tiles, CHIPS, split_axis=0, concat_axis=0, tiled=True)]
    unnamed x19 -> x8, local copies, waits for them, and re-layouts: 17 us -> 3.02 us
    ppermute x16, waiting for transfers between devices: 28.8 us -> 17.3 us  [local(): arriving = lax.ppermute(made, 'section', back)]
  transfers between devices with their start and end apart: 36 -> 54, of which waited for: 18 -> 21; matrix products, arithmetic and copies ran while one was open for 2% -> 0% of each run, Pallas kernels for 20% -> 24%
where the time goes in v1:
time: 441 us; the launch traced here: 433 us
  Pallas kernels  174 us (39%)
  starting transfers between devices  142 us (32%)
  waiting for transfers between devices  106 us (24%)
  local copies, waits for them, and re-layouts  7.32 us (2%)
    pallas_call x17, Pallas kernels, forward_step(): pl.pallas_call(functools.partial(forward_body, tick, micro), out_shape=(j...  87 us
    pallas_call x17, Pallas kernels, backward_step(): pl.pallas_call(functools.partial(backward_body, tick, micro, last), out_s...  70.5 us
    ppermute x16, starting transfers between devices, local(): arriving = lax.ppermute(made, 'section', back)  59.2 us
    ppermute x16, waiting for transfers between devices, local(): came = lax.ppermute(made, 'section', onward)  54.8 us
    ppermute x21, starting transfers between devices, hand_round(): lax.ppermute(tiles[d], CHIPS, [(i, (i + d) % chips) for i in range(chips)])  49 us
    ppermute x21, waiting for transfers between devices, hand_round(): lax.ppermute(tiles[d], CHIPS, [(i, (i + d) % chips) for i in range(chips)])  31.9 us
    ppermute x1, starting transfers between devices, local(): theirs = lax.ppermute(theirs, CORE, [(0, 1), (1, 0)])  29.9 us
    ppermute x16, waiting for transfers between devices, local(): arriving = lax.ppermute(made, 'section', back)  17.3 us
  transfers between devices with their start and end apart: 54, of which 21 were waited for; matrix products, arithmetic and copies ran while one was open for 0% of the time, Pallas kernels for 24%

profile of v1, /device:TPU:1, one launch (start us, length us, event | category | flops | bytes accessed | tf_op | source)
XLA Modules:
  0.0 432.9 jit_solution(6749989456407543330)
XLA Ops:
  5.0 10.9 %forward_step.17 = (bf16[16,8192]{1,0:T(8,128)(2,1)S(1)}, bf16[8,11,16,1024]{3,2,1,0:T(8,128)(2,1)S(1)}, f32[11,16,640]{2,1,0:T(8,128)S(1)}, bf16[8192,512]{1,0:T(8,128)(2,1)S(1)}, bf16[8192,512]{1,0:T(8,128)(2,1)S(1)}) custom-call(s32[38]{0:T(128)S(1)} %concatenate.7.refs_0_.ctl_ref, bf16[160,8192]{1,0:T(8,128)(2,1)} %refs_1_.25, ...), custom_call_target="tpu_custom_call" | custom-call | tf_op jit(solution)/shard_map/forward_step/pallas_call | solution.py:112
  18.5 9.1 %collective-permute-done.refs_5_ = bf16[16,8192]{1,0:T(8,128)(2,1)S(1)} collective-permute-done((bf16[16,8192]{1,0:T(8,128)(2,1)S(1)}, bf16[16,8192]{1,0:T(8,128)(2,1)S(1)}, u32[]{:S(2)}, u32[]{:S(2)}) %collective-permute-start) | collective-permute-done | bytes 262176 | tf_op jit(solution)/shard_map/ppermute | solution.py:323
  27.6 5.1 %forward_step.18 = (bf16[16,8192]{1,0:T(8,128)(2,1)S(1)}, bf16[8,11,16,1024]{3,2,1,0:T(8,128)(2,1)S(1)}, f32[11,16,640]{2,1,0:T(8,128)S(1)}, bf16[8192,512]{1,0:T(8,128)(2,1)S(1)}, bf16[8192,512]{1,0:T(8,128)(2,1)S(1)}) custom-call(s32[38]{0:T(128)S(1)} %concatenate.7.refs_0_.ctl_ref, ...), custom_call_target="tpu_custom_call", output_to_operand_aliasing={{3}: (2, {}), {4}: (3, {}), {1}: (6, {}), {2}: (7, {})} | custom-call | tf_op jit(solution)/shard_map/forward_step/pallas_call | solution.py:112
  32.8 8.7 %collective-permute-done.1.refs_5_ = bf16[16,8192]{1,0:T(8,128)(2,1)S(1)} collective-permute-done((bf16[16,8192]{1,0:T(8,128)(2,1)S(1)}, bf16[16,8192]{1,0:T(8,128)(2,1)S(1)}, u32[]{:S(2)}, u32[]{:S(2)}) %collective-permute-start.1) | collective-permute-done | bytes 262176 | tf_op jit(solution)/shard_map/ppermute | solution.py:323
  41.4 5.1 %forward_step.19 = (bf16[16,8192]{1,0:T(8,128)(2,1)S(1)}, bf16[8,11,16,1024]{3,2,1,0:T(8,128)(2,1)S(1)}, f32[11,16,640]{2,1,0:T(8,128)S(1)}, bf16[8192,512]{1,0:T(8,128)(2,1)S(1)}, bf16[8192,512]{1,0:T(8,128)(2,1)S(1)}) custom-call(s32[38]{0:T(128)S(1)} %concatenate.7.refs_0_.ctl_ref, ...), custom_call_target="tpu_custom_call", output_to_operand_aliasing={{3}: (2, {}), {4}: (3, {}), {1}: (6, {}), {2}: (7, {})} | custom-call | tf_op jit(solution)/shard_map/forward_step/pallas_call | solution.py:112
  46.6 7.7 %collective-permute-done.2.refs_5_ = bf16[16,8192]{1,0:T(8,128)(2,1)S(1)} collective-permute-done((bf16[16,8192]{1,0:T(8,128)(2,1)S(1)}, bf16[16,8192]{1,0:T(8,128)(2,1)S(1)}, u32[]{:S(2)}, u32[]{:S(2)}) %collective-permute-start.2) | collective-permute-done | bytes 262176 | tf_op jit(solution)/shard_map/ppermute | solution.py:323
  54.4 5.1 %forward_step.20 = (bf16[16,8192]{1,0:T(8,128)(2,1)S(1)}, bf16[8,11,16,1024]{3,2,1,0:T(8,128)(2,1)S(1)}, f32[11,16,640]{2,1,0:T(8,128)S(1)}, bf16[8192,512]{1,0:T(8,128)(2,1)S(1)}, bf16[8192,512]{1,0:T(8,128)(2,1)S(1)}) custom-call(s32[38]{0:T(128)S(1)} %concatenate.7.refs_0_.ctl_ref, ...), custom_call_target="tpu_custom_call", output_to_operand_aliasing={{3}: (2, {}), {4}: (3, {}), {1}: (6, {}), {2}: (7, {})} | custom-call | tf_op jit(solution)/shard_map/forward_step/pallas_call | solution.py:112
  59.6 7.3 %collective-permute-done.3.refs_5_ = bf16[16,8192]{1,0:T(8,128)(2,1)S(1)} collective-permute-done((bf16[16,8192]{1,0:T(8,128)(2,1)S(1)}, bf16[16,8192]{1,0:T(8,128)(2,1)S(1)}, u32[]{:S(2)}, u32[]{:S(2)}) %collective-permute-start.3) | collective-permute-done | bytes 262176 | tf_op jit(solution)/shard_map/ppermute | solution.py:323
  66.9 5.1 %forward_step.21 = (bf16[16,8192]{1,0:T(8,128)(2,1)S(1)}, bf16[8,11,16,1024]{3,2,1,0:T(8,128)(2,1)S(1)}, f32[11,16,640]{2,1,0:T(8,128)S(1)}, bf16[8192,512]{1,0:T(8,128)(2,1)S(1)}, bf16[8192,512]{1,0:T(8,128)(2,1)S(1)}) custom-call(s32[38]{0:T(128)S(1)} %concatenate.7.refs_0_.ctl_ref, ...), custom_call_target="tpu_custom_call", output_to_operand_aliasing={{3}: (2, {}), {4}: (3, {}), {1}: (6, {}), {2}: (7, {})} | custom-call | tf_op jit(solution)/shard_map/forward_step/pallas_call | solution.py:112
  72.1 7.3 %collective-permute-done.4.refs_5_ = bf16[16,8192]{1,0:T(8,128)(2,1)S(1)} collective-permute-done((bf16[16,8192]{1,0:T(8,128)(2,1)S(1)}, bf16[16,8192]{1,0:T(8,128)(2,1)S(1)}, u32[]{:S(2)}, u32[]{:S(2)}) %collective-permute-start.4) | collective-permute-done | bytes 262176 | tf_op jit(solution)/shard_map/ppermute | solution.py:323
  79.4 5.5 %forward_step.22 = (bf16[16,8192]{1,0:T(8,128)(2,1)S(1)}, bf16[8,11,16,1024]{3,2,1,0:T(8,128)(2,1)S(1)}, f32[11,16,640]{2,1,0:T(8,128)S(1)}, bf16[8192,512]{1,0:T(8,128)(2,1)S(1)}, bf16[8192,512]{1,0:T(8,128)(2,1)S(1)}) custom-call(s32[38]{0:T(128)S(1)} %concatenate.7.refs_0_.ctl_ref, ...), custom_call_target="tpu_custom_call", output_to_operand_aliasing={{3}: (2, {}), {4}: (3, {}), {1}: (6, {}), {2}: (7, {})} | custom-call | tf_op jit(solution)/shard_map/forward_step/pallas_call | solution.py:112
  85.0 7.3 %collective-permute-done.5.refs_5_ = bf16[16,8192]{1,0:T(8,128)(2,1)S(1)} collective-permute-done((bf16[16,8192]{1,0:T(8,128)(2,1)S(1)}, bf16[16,8192]{1,0:T(8,128)(2,1)S(1)}, u32[]{:S(2)}, u32[]{:S(2)}) %collective-permute-start.5) | collective-permute-done | bytes 262176 | tf_op jit(solution)/shard_map/ppermute | solution.py:323
  92.4 5.1 %forward_step.23 = (bf16[16,8192]{1,0:T(8,128)(2,1)S(1)}, bf16[8,11,16,1024]{3,2,1,0:T(8,128)(2,1)S(1)}, f32[11,16,640]{2,1,0:T(8,128)S(1)}, bf16[8192,512]{1,0:T(8,128)(2,1)S(1)}, bf16[8192,512]{1,0:T(8,128)(2,1)S(1)}) custom-call(s32[38]{0:T(128)S(1)} %concatenate.7.refs_0_.ctl_ref, ...), custom_call_target="tpu_custom_call", output_to_operand_aliasing={{3}: (2, {}), {4}: (3, {}), {1}: (6, {}), {2}: (7, {})} | custom-call | tf_op jit(solution)/shard_map/forward_step/pallas_call | solution.py:112
  97.6 7.3 %collective-permute-done.6.refs_5_ = bf16[16,8192]{1,0:T(8,128)(2,1)S(1)} collective-permute-done((bf16[16,8192]{1,0:T(8,128)(2,1)S(1)}, bf16[16,8192]{1,0:T(8,128)(2,1)S(1)}, u32[]{:S(2)}, u32[]{:S(2)}) %collective-permute-start.6) | collective-permute-done | bytes 262176 | tf_op jit(solution)/shard_map/ppermute | solution.py:323
  104.9 5.1 %forward_step.24 = (bf16[16,8192]{1,0:T(8,128)(2,1)S(1)}, bf16[8,11,16,1024]{3,2,1,0:T(8,128)(2,1)S(1)}, f32[11,16,640]{2,1,0:T(8,128)S(1)}, bf16[8192,512]{1,0:T(8,128)(2,1)S(1)}, bf16[8192,512]{1,0:T(8,128)(2,1)S(1)}) custom-call(s32[38]{0:T(128)S(1)} %concatenate.7.refs_0_.ctl_ref, ...), custom_call_target="tpu_custom_call", output_to_operand_aliasing={{3}: (2, {}), {4}: (3, {}), {1}: (6, {}), {2}: (7, {})} | custom-call | tf_op jit(solution)/shard_map/forward_step/pallas_call | solution.py:112
  118.7 5.1 %forward_step.25 = (bf16[16,8192]{1,0:T(8,128)(2,1)S(1)}, bf16[8,11,16,1024]{3,2,1,0:T(8,128)(2,1)S(1)}, f32[11,16,640]{2,1,0:T(8,128)S(1)}, bf16[8192,512]{1,0:T(8,128)(2,1)S(1)}, bf16[8192,512]{1,0:T(8,128)(2,1)S(1)}) custom-call(s32[38]{0:T(128)S(1)} %concatenate.7.refs_0_.ctl_ref, ...), custom_call_target="tpu_custom_call", output_to_operand_aliasing={{3}: (2, {}), {4}: (3, {}), {1}: (6, {}), {2}: (7, {})} | custom-call | tf_op jit(solution)/shard_map/forward_step/pallas_call | solution.py:112
  132.6 5.1 %forward_step.26 = (bf16[16,8192]{1,0:T(8,128)(2,1)S(1)}, bf16[8,11,16,1024]{3,2,1,0:T(8,128)(2,1)S(1)}, f32[11,16,640]{2,1,0:T(8,128)S(1)}, bf16[8192,512]{1,0:T(8,128)(2,1)S(1)}, bf16[8192,512]{1,0:T(8,128)(2,1)S(1)}) custom-call(s32[38]{0:T(128)S(1)} %concatenate.7.refs_0_.ctl_ref, ...), custom_call_target="tpu_custom_call", output_to_operand_aliasing={{3}: (2, {}), {4}: (3, {}), {1}: (6, {}), {2}: (7, {})} | custom-call | tf_op jit(solution)/shard_map/forward_step/pallas_call | solution.py:112
  207.9 5.0 %collective-permute-start.22 = (bf16[16,8192]{1,0:T(8,128)(2,1)S(1)}, bf16[16,8192]{1,0:T(8,128)(2,1)S(1)}, u32[]{:S(2)}, u32[]{:S(2)}) collective-permute-start(bf16[16,8192]{1,0:T(8,128)(2,1)S(1)} %get-tuple-element.335), channel_id=1, source_target_pairs={{1,0},{2,1},{3,2},{4,3},{5,4},{6,5},{7,6},{0,7},{9,8},{10,9},{11,1... | collective-permute-start | bytes 786440 | tf_op jit(solution)/shard_map/ppermute | solution.py:333
  222.8 5.5 %collective-permute-start.24 = (bf16[16,8192]{1,0:T(8,128)(2,1)S(1)}, bf16[16,8192]{1,0:T(8,128)(2,1)S(1)}, u32[]{:S(2)}, u32[]{:S(2)}) collective-permute-start(bf16[16,8192]{1,0:T(8,128)(2,1)S(1)} %get-tuple-element.346), channel_id=1, source_target_pairs={{1,0},{2,1},{3,2},{4,3},{5,4},{6,5},{7,6},{0,7},{9,8},{10,9},{11,1... | collective-permute-start | bytes 786440 | tf_op jit(solution)/shard_map/ppermute | solution.py:333
  237.4 5.3 %collective-permute-start.25 = (bf16[16,8192]{1,0:T(8,128)(2,1)S(1)}, bf16[16,8192]{1,0:T(8,128)(2,1)S(1)}, u32[]{:S(2)}, u32[]{:S(2)}) collective-permute-start(bf16[16,8192]{1,0:T(8,128)(2,1)S(1)} %get-tuple-element.352), channel_id=1, source_target_pairs={{1,0},{2,1},{3,2},{4,3},{5,4},{6,5},{7,6},{0,7},{9,8},{10,9},{11,1... | collective-permute-start | bytes 786440 | tf_op jit(solution)/shard_map/ppermute | solution.py:333
  255.2 5.0 %collective-permute-start.34 = (bf16[160,1024]{1,0:T(8,128)(2,1)S(1)}, bf16[160,1024]{1,0:T(8,128)(2,1)S(1)}, u32[]{:S(2)}, u32[]{:S(2)}) collective-permute-start(bf16[160,1024]{1,0:T(8,128)(2,1)S(1)} %bitcast.55), channel_id=1, source_target_pairs={{0,96},{16,112},{32,0},{48,16},{64,32},{80,48},{96,64},{112,80},{1... | collective-permute-start | bytes 983048 | tf_op jit(solution)/shard_map/ppermute | solution.py:309
  290.2 5.9 %collective-permute-done.30.refs_2_ = bf16[160,1024]{1,0:T(8,128)(2,1)S(1)} collective-permute-done((bf16[160,1024]{1,0:T(8,128)(2,1)S(1)}, bf16[160,1024]{1,0:T(8,128)(2,1)S(1)}, u32[]{:S(2)}, u32[]{:S(2)}) %collective-permute-start.30) | collective-permute-done | bytes 327712 | tf_op jit(solution)/shard_map/ppermute | solution.py:309
  300.6 5.1 %collective-permute-done.36.refs_7_ = bf16[16,8192]{1,0:T(8,128)(2,1)S(1)} collective-permute-done((bf16[16,8192]{1,0:T(8,128)(2,1)S(1)}, bf16[16,8192]{1,0:T(8,128)(2,1)S(1)}, u32[]{:S(2)}, u32[]{:S(2)}) %collective-permute-start.36) | collective-permute-done | bytes 262176 | tf_op jit(solution)/shard_map/ppermute | solution.py:333
  313.8 6.5 %collective-permute-start.51 = (bf16[112,2048]{1,0:T(8,128)(2,1)S(1)}, bf16[112,2048]{1,0:T(8,128)(2,1)S(1)}, u32[]{:S(2)}, u32[]{:S(2)}) collective-permute-start(bf16[112,2048]{1,0:T(8,128)(2,1)S(1)} %bitcast.48), channel_id=1, source_target_pairs={{0,96},{16,112},{32,0},{48,16},{64,32},{80,48},{96,64},{112,80},{1... | collective-permute-start | bytes 1376264 | tf_op jit(solution)/shard_map/ppermute | solution.py:309
  325.2 5.4 %collective-permute-start.50 = (bf16[112,2048]{1,0:T(8,128)(2,1)S(1)}, bf16[112,2048]{1,0:T(8,128)(2,1)S(1)}, u32[]{:S(2)}, u32[]{:S(2)}) collective-permute-start(bf16[112,2048]{1,0:T(8,128)(2,1)S(1)} %bitcast.46), channel_id=1, source_target_pairs={{0,80},{16,96},{32,112},{48,0},{64,16},{80,32},{96,48},{112,64},{1... | collective-permute-start | bytes 1376264 | tf_op jit(solution)/shard_map/ppermute | solution.py:309
  330.6 5.7 %collective-permute-done.38.refs_7_ = bf16[16,8192]{1,0:T(8,128)(2,1)S(1)} collective-permute-done((bf16[16,8192]{1,0:T(8,128)(2,1)S(1)}, bf16[16,8192]{1,0:T(8,128)(2,1)S(1)}, u32[]{:S(2)}, u32[]{:S(2)}) %collective-permute-start.38) | collective-permute-done | bytes 262176 | tf_op jit(solution)/shard_map/ppermute | solution.py:333
  347.1 6.0 %collective-permute-start.44 = (bf16[48,2048]{1,0:T(8,128)(2,1)S(1)}, bf16[48,2048]{1,0:T(8,128)(2,1)S(1)}, u32[]{:S(2)}, u32[]{:S(2)}) collective-permute-start(bf16[48,2048]{1,0:T(8,128)(2,1)S(1)} %bitcast.62), channel_id=1, source_target_pairs={{0,96},{16,112},{32,0},{48,16},{64,32},{80,48},{96,64},{112,80},{1... | collective-permute-start | bytes 589832 | tf_op jit(solution)/shard_map/ppermute | solution.py:309
  353.0 7.7 %collective-permute-done.49.refs_12_ = bf16[112,2048]{1,0:T(8,128)(2,1)S(1)} collective-permute-done((bf16[112,2048]{1,0:T(8,128)(2,1)S(1)}, bf16[112,2048]{1,0:T(8,128)(2,1)S(1)}, u32[]{:S(2)}, u32[]{:S(2)}) %collective-permute-start.49) | collective-permute-done | bytes 458784 | tf_op jit(solution)/shard_map/ppermute | solution.py:309
  364.6 6.8 %collective-permute-start.42 = (bf16[48,2048]{1,0:T(8,128)(2,1)S(1)}, bf16[48,2048]{1,0:T(8,128)(2,1)S(1)}, u32[]{:S(2)}, u32[]{:S(2)}) collective-permute-start(bf16[48,2048]{1,0:T(8,128)(2,1)S(1)} %bitcast.59), channel_id=1, source_target_pairs={{0,64},{16,80},{32,96},{48,112},{64,0},{80,16},{96,32},{112,48},{1... | collective-permute-start | bytes 589832 | tf_op jit(solution)/shard_map/ppermute | solution.py:309
  374.1 7.7 %gradient_step.2.refs_16_ = f32[1024,1024]{1,0:T(8,128)S(1)} custom-call(s32[38]{0:T(128)S(1)} %concatenate.7.refs_0_.ctl_ref, bf16[160,1024]{1,0:T(8,128)(2,1)S(1)} %bitcast.36, bf16[160,1024]{1,0:T(8,128)(2,1)S(1)} %collective-permute-done.29.refs_1_, bf16[160,1024]{1,0:T(8,128)(2,1)S(1)} %collective-permute-done.30.refs_2_, ...), custom_call_target="tpu_custom_call" | custom-call | tf_op jit(solution)/shard_map/gradient_step/pallas_call | solution.py:254
  387.5 5.1 %gradient_step.3 = (f32[512,1024]{1,0:T(8,128)S(1)}, bf16[512,1024]{1,0:T(8,128)(2,1)S(1)}) custom-call(s32[38]{0:T(128)S(1)} %concatenate.7.refs_0_.ctl_ref, bf16[160,1024]{1,0:T(8,128)(2,1)S(1)} %bitcast.37, bf16[160,1024]{1,0:T(8,128)(2,1)S(1)} %collective-permute-done.29.refs_1_, bf16[160,1024]{1,0:T(8,128)(2,1)S(1)} %collective-permute-done.30.refs_2_, ...), custom_call_target="tpu_custom_call" | custom-call | tf_op jit(solution)/shard_map/gradient_step/pallas_call | solution.py:254
  394.0 29.9 %collective-permute-start.53 = (bf16[512,1024]{1,0:T(8,128)(2,1)S(1)}, bf16[512,1024]{1,0:T(8,128)(2,1)S(1)}, u32[]{:S(2)}, u32[]{:S(2)}) collective-permute-start(bf16[512,1024]{1,0:T(8,128)(2,1)S(1)} %get-tuple-element.401), channel_id=1, source_target_pairs={{0,8},{8,0},{1,9},{9,1},{2,10},{10,2},{3,11},{11,3},{4,12},{12,4},... | collective-permute-start | bytes 3145736 | tf_op jit(solution)/shard_map/ppermute | solution.py:340
  (131 shorter events, 206.5 us)
Async XLA Ops:
  16.0 11.6 %collective-permute-start = (bf16[16,8192]{1,0:T(8,128)(2,1)S(1)}, bf16[16,8192]{1,0:T(8,128)(2,1)S(1)}, u32[]{:S(2)}, u32[]{:S(2)}) collective-permute-start(bf16[16,8192]{1,0:T(8,128)(2,1)S(1)} %get-tuple-element.212), channel_id=1, source_target_pairs={{0,1},{1,2},{2,3},{3,4},{4,5},{5,6},{6,7},{7,0},{8,9},{9,10},{10,1... | collective-permute-start | bytes 786440 | tf_op jit(solution)/shard_map/ppermute | solution.py:323
  193.9 10.0 %collective-permute-start.20 = (bf16[16,8192]{1,0:T(8,128)(2,1)S(1)}, bf16[16,8192]{1,0:T(8,128)(2,1)S(1)}, u32[]{:S(2)}, u32[]{:S(2)}) collective-permute-start(bf16[16,8192]{1,0:T(8,128)(2,1)S(1)} %get-tuple-element.324), channel_id=1, source_target_pairs={{1,0},{2,1},{3,2},{4,3},{5,4},{6,5},{7,6},{0,7},{9,8},{10,9},{11,1... | collective-permute-start | bytes 786440 | tf_op jit(solution)/shard_map/ppermute | solution.py:333
  207.9 10.8 %collective-permute-start.22 = (bf16[16,8192]{1,0:T(8,128)(2,1)S(1)}, bf16[16,8192]{1,0:T(8,128)(2,1)S(1)}, u32[]{:S(2)}, u32[]{:S(2)}) collective-permute-start(bf16[16,8192]{1,0:T(8,128)(2,1)S(1)} %get-tuple-element.335), channel_id=1, source_target_pairs={{1,0},{2,1},{3,2},{4,3},{5,4},{6,5},{7,6},{0,7},{9,8},{10,9},{11,1... | collective-permute-start | bytes 786440 | tf_op jit(solution)/shard_map/ppermute | solution.py:333
  217.1 11.2 %collective-permute-start.23 = (bf16[16,8192]{1,0:T(8,128)(2,1)S(1)}, bf16[16,8192]{1,0:T(8,128)(2,1)S(1)}, u32[]{:S(2)}, u32[]{:S(2)}) collective-permute-start(bf16[16,8192]{1,0:T(8,128)(2,1)S(1)} %get-tuple-element.339), channel_id=1, source_target_pairs={{0,1},{1,2},{2,3},{3,4},{4,5},{5,6},{6,7},{7,0},{8,9},{9,10},{10,1... | collective-permute-start | bytes 786440 | tf_op jit(solution)/shard_map/ppermute | solution.py:323
  222.8 10.6 %collective-permute-start.24 = (bf16[16,8192]{1,0:T(8,128)(2,1)S(1)}, bf16[16,8192]{1,0:T(8,128)(2,1)S(1)}, u32[]{:S(2)}, u32[]{:S(2)}) collective-permute-start(bf16[16,8192]{1,0:T(8,128)(2,1)S(1)} %get-tuple-element.346), channel_id=1, source_target_pairs={{1,0},{2,1},{3,2},{4,3},{5,4},{6,5},{7,6},{0,7},{9,8},{10,9},{11,1... | collective-permute-start | bytes 786440 | tf_op jit(solution)/shard_map/ppermute | solution.py:333
  250.8 10.2 %collective-permute-start.26 = (bf16[16,8192]{1,0:T(8,128)(2,1)S(1)}, bf16[16,8192]{1,0:T(8,128)(2,1)S(1)}, u32[]{:S(2)}, u32[]{:S(2)}) collective-permute-start(bf16[16,8192]{1,0:T(8,128)(2,1)S(1)} %get-tuple-element.358), channel_id=1, source_target_pairs={{1,0},{2,1},{3,2},{4,3},{5,4},{6,5},{7,6},{0,7},{9,8},{10,9},{11,1... | collective-permute-start | bytes 786440 | tf_op jit(solution)/shard_map/ppermute | solution.py:333
  255.2 15.4 %collective-permute-start.34 = (bf16[160,1024]{1,0:T(8,128)(2,1)S(1)}, bf16[160,1024]{1,0:T(8,128)(2,1)S(1)}, u32[]{:S(2)}, u32[]{:S(2)}) collective-permute-start(bf16[160,1024]{1,0:T(8,128)(2,1)S(1)} %bitcast.55), channel_id=1, source_target_pairs={{0,96},{16,112},{32,0},{48,16},{64,32},{80,48},{96,64},{112,80},{1... | collective-permute-start | bytes 983048 | tf_op jit(solution)/shard_map/ppermute | solution.py:309
  260.2 11.5 %collective-permute-start.35 = (bf16[160,1024]{1,0:T(8,128)(2,1)S(1)}, bf16[160,1024]{1,0:T(8,128)(2,1)S(1)}, u32[]{:S(2)}, u32[]{:S(2)}) collective-permute-start(bf16[160,1024]{1,0:T(8,128)(2,1)S(1)} %bitcast.54), channel_id=1, source_target_pairs={{0,112},{16,0},{32,16},{48,32},{64,48},{80,64},{96,80},{112,96},{1... | collective-permute-start | bytes 983048 | tf_op jit(solution)/shard_map/ppermute | solution.py:309
  265.0 10.7 %collective-permute-start.27 = (bf16[16,8192]{1,0:T(8,128)(2,1)S(1)}, bf16[16,8192]{1,0:T(8,128)(2,1)S(1)}, u32[]{:S(2)}, u32[]{:S(2)}) collective-permute-start(bf16[16,8192]{1,0:T(8,128)(2,1)S(1)} %get-tuple-element.364), channel_id=1, source_target_pairs={{1,0},{2,1},{3,2},{4,3},{5,4},{6,5},{7,6},{0,7},{9,8},{10,9},{11,1... | collective-permute-start | bytes 786440 | tf_op jit(solution)/shard_map/ppermute | solution.py:333
  266.6 13.8 %collective-permute-start.33 = (bf16[160,1024]{1,0:T(8,128)(2,1)S(1)}, bf16[160,1024]{1,0:T(8,128)(2,1)S(1)}, u32[]{:S(2)}, u32[]{:S(2)}) collective-permute-start(bf16[160,1024]{1,0:T(8,128)(2,1)S(1)} %bitcast.53), channel_id=1, source_target_pairs={{0,80},{16,96},{32,112},{48,0},{64,16},{80,32},{96,48},{112,64},{1... | collective-permute-start | bytes 983048 | tf_op jit(solution)/shard_map/ppermute | solution.py:309
  270.0 16.3 %collective-permute-start.32 = (bf16[160,1024]{1,0:T(8,128)(2,1)S(1)}, bf16[160,1024]{1,0:T(8,128)(2,1)S(1)}, u32[]{:S(2)}, u32[]{:S(2)}) collective-permute-start(bf16[160,1024]{1,0:T(8,128)(2,1)S(1)} %bitcast.52), channel_id=1, source_target_pairs={{0,64},{16,80},{32,96},{48,112},{64,0},{80,16},{96,32},{112,48},{1... | collective-permute-start | bytes 983048 | tf_op jit(solution)/shard_map/ppermute | solution.py:309
  270.6 19.7 %collective-permute-start.31 = (bf16[160,1024]{1,0:T(8,128)(2,1)S(1)}, bf16[160,1024]{1,0:T(8,128)(2,1)S(1)}, u32[]{:S(2)}, u32[]{:S(2)}) collective-permute-start(bf16[160,1024]{1,0:T(8,128)(2,1)S(1)} %bitcast.51), channel_id=1, source_target_pairs={{0,48},{16,64},{32,80},{48,96},{64,112},{80,0},{96,16},{112,32},{1... | collective-permute-start | bytes 983048 | tf_op jit(solution)/shard_map/ppermute | solution.py:309
  271.7 24.4 %collective-permute-start.30 = (bf16[160,1024]{1,0:T(8,128)(2,1)S(1)}, bf16[160,1024]{1,0:T(8,128)(2,1)S(1)}, u32[]{:S(2)}, u32[]{:S(2)}) collective-permute-start(bf16[160,1024]{1,0:T(8,128)(2,1)S(1)} %bitcast.50), channel_id=1, source_target_pairs={{0,32},{16,48},{32,64},{48,80},{64,96},{80,112},{96,0},{112,16},{1... | collective-permute-start | bytes 983048 | tf_op jit(solution)/shard_map/ppermute | solution.py:309
  275.8 20.3 %collective-permute-start.29 = (bf16[160,1024]{1,0:T(8,128)(2,1)S(1)}, bf16[160,1024]{1,0:T(8,128)(2,1)S(1)}, u32[]{:S(2)}, u32[]{:S(2)}) collective-permute-start(bf16[160,1024]{1,0:T(8,128)(2,1)S(1)} %bitcast.49), channel_id=1, source_target_pairs={{0,16},{16,32},{32,48},{48,64},{64,80},{80,96},{96,112},{112,0},{1... | collective-permute-start | bytes 983048 | tf_op jit(solution)/shard_map/ppermute | solution.py:309
  280.4 15.7 %collective-permute-start.28 = (bf16[16,8192]{1,0:T(8,128)(2,1)S(1)}, bf16[16,8192]{1,0:T(8,128)(2,1)S(1)}, u32[]{:S(2)}, u32[]{:S(2)}) collective-permute-start(bf16[16,8192]{1,0:T(8,128)(2,1)S(1)} %get-tuple-element.366), channel_id=1, source_target_pairs={{1,0},{2,1},{3,2},{4,3},{5,4},{6,5},{7,6},{0,7},{9,8},{10,9},{11,1... | collective-permute-start | bytes 786440 | tf_op jit(solution)/shard_map/ppermute | solution.py:333
  309.7 10.6 %collective-permute-start.37 = (bf16[16,8192]{1,0:T(8,128)(2,1)S(1)}, bf16[16,8192]{1,0:T(8,128)(2,1)S(1)}, u32[]{:S(2)}, u32[]{:S(2)}) collective-permute-start(bf16[16,8192]{1,0:T(8,128)(2,1)S(1)} %get-tuple-element.391), channel_id=1, source_target_pairs={{1,0},{2,1},{3,2},{4,3},{5,4},{6,5},{7,6},{0,7},{9,8},{10,9},{11,1... | collective-permute-start | bytes 786440 | tf_op jit(solution)/shard_map/ppermute | solution.py:333
  313.8 27.5 %collective-permute-start.51 = (bf16[112,2048]{1,0:T(8,128)(2,1)S(1)}, bf16[112,2048]{1,0:T(8,128)(2,1)S(1)}, u32[]{:S(2)}, u32[]{:S(2)}) collective-permute-start(bf16[112,2048]{1,0:T(8,128)(2,1)S(1)} %bitcast.48), channel_id=1, source_target_pairs={{0,96},{16,112},{32,0},{48,16},{64,32},{80,48},{96,64},{112,80},{1... | collective-permute-start | bytes 1376264 | tf_op jit(solution)/shard_map/ppermute | solution.py:309
  320.3 23.1 %collective-permute-start.52 = (bf16[112,2048]{1,0:T(8,128)(2,1)S(1)}, bf16[112,2048]{1,0:T(8,128)(2,1)S(1)}, u32[]{:S(2)}, u32[]{:S(2)}) collective-permute-start(bf16[112,2048]{1,0:T(8,128)(2,1)S(1)} %bitcast.47), channel_id=1, source_target_pairs={{0,112},{16,0},{32,16},{48,32},{64,48},{80,64},{96,80},{112,96},{1... | collective-permute-start | bytes 1376264 | tf_op jit(solution)/shard_map/ppermute | solution.py:309
  324.3 11.9 %collective-permute-start.38 = (bf16[16,8192]{1,0:T(8,128)(2,1)S(1)}, bf16[16,8192]{1,0:T(8,128)(2,1)S(1)}, u32[]{:S(2)}, u32[]{:S(2)}) collective-permute-start(bf16[16,8192]{1,0:T(8,128)(2,1)S(1)} %get-tuple-element.397), channel_id=1, source_target_pairs={{1,0},{2,1},{3,2},{4,3},{5,4},{6,5},{7,6},{0,7},{9,8},{10,9},{11,1... | collective-permute-start | bytes 786440 | tf_op jit(solution)/shard_map/ppermute | solution.py:333
  325.2 21.9 %collective-permute-start.50 = (bf16[112,2048]{1,0:T(8,128)(2,1)S(1)}, bf16[112,2048]{1,0:T(8,128)(2,1)S(1)}, u32[]{:S(2)}, u32[]{:S(2)}) collective-permute-start(bf16[112,2048]{1,0:T(8,128)(2,1)S(1)} %bitcast.46), channel_id=1, source_target_pairs={{0,80},{16,96},{32,112},{48,0},{64,16},{80,32},{96,48},{112,64},{1... | collective-permute-start | bytes 1376264 | tf_op jit(solution)/shard_map/ppermute | solution.py:309
  330.6 30.2 %collective-permute-start.49 = (bf16[112,2048]{1,0:T(8,128)(2,1)S(1)}, bf16[112,2048]{1,0:T(8,128)(2,1)S(1)}, u32[]{:S(2)}, u32[]{:S(2)}) collective-permute-start(bf16[112,2048]{1,0:T(8,128)(2,1)S(1)} %bitcast.45), channel_id=1, source_target_pairs={{0,64},{16,80},{32,96},{48,112},{64,0},{80,16},{96,32},{112,48},{1... | collective-permute-start | bytes 1376264 | tf_op jit(solution)/shard_map/ppermute | solution.py:309
  336.3 28.3 %collective-permute-start.48 = (bf16[112,2048]{1,0:T(8,128)(2,1)S(1)}, bf16[112,2048]{1,0:T(8,128)(2,1)S(1)}, u32[]{:S(2)}, u32[]{:S(2)}) collective-permute-start(bf16[112,2048]{1,0:T(8,128)(2,1)S(1)} %bitcast.44), channel_id=1, source_target_pairs={{0,48},{16,64},{32,80},{48,96},{64,112},{80,0},{96,16},{112,32},{1... | collective-permute-start | bytes 1376264 | tf_op jit(solution)/shard_map/ppermute | solution.py:309
  341.2 23.3 %collective-permute-start.47 = (bf16[112,2048]{1,0:T(8,128)(2,1)S(1)}, bf16[112,2048]{1,0:T(8,128)(2,1)S(1)}, u32[]{:S(2)}, u32[]{:S(2)}) collective-permute-start(bf16[112,2048]{1,0:T(8,128)(2,1)S(1)} %bitcast.43), channel_id=1, source_target_pairs={{0,32},{16,48},{32,64},{48,80},{64,96},{80,112},{96,0},{112,16},{1... | collective-permute-start | bytes 1376264 | tf_op jit(solution)/shard_map/ppermute | solution.py:309
  343.4 28.0 %collective-permute-start.46 = (bf16[112,2048]{1,0:T(8,128)(2,1)S(1)}, bf16[112,2048]{1,0:T(8,128)(2,1)S(1)}, u32[]{:S(2)}, u32[]{:S(2)}) collective-permute-start(bf16[112,2048]{1,0:T(8,128)(2,1)S(1)} %bitcast.42), channel_id=1, source_target_pairs={{0,16},{16,32},{32,48},{48,64},{64,80},{80,96},{96,112},{112,0},{1... | collective-permute-start | bytes 1376264 | tf_op jit(solution)/shard_map/ppermute | solution.py:309
  347.1 25.0 %collective-permute-start.44 = (bf16[48,2048]{1,0:T(8,128)(2,1)S(1)}, bf16[48,2048]{1,0:T(8,128)(2,1)S(1)}, u32[]{:S(2)}, u32[]{:S(2)}) collective-permute-start(bf16[48,2048]{1,0:T(8,128)(2,1)S(1)} %bitcast.62), channel_id=1, source_target_pairs={{0,96},{16,112},{32,0},{48,16},{64,32},{80,48},{96,64},{112,80},{1... | collective-permute-start | bytes 589832 | tf_op jit(solution)/shard_map/ppermute | solution.py:309
  360.7 11.8 %collective-permute-start.45 = (bf16[48,2048]{1,0:T(8,128)(2,1)S(1)}, bf16[48,2048]{1,0:T(8,128)(2,1)S(1)}, u32[]{:S(2)}, u32[]{:S(2)}) collective-permute-start(bf16[48,2048]{1,0:T(8,128)(2,1)S(1)} %bitcast.61), channel_id=1, source_target_pairs={{0,112},{16,0},{32,16},{48,32},{64,48},{80,64},{96,80},{112,96},{1... | collective-permute-start | bytes 589832 | tf_op jit(solution)/shard_map/ppermute | solution.py:309
  364.6 17.3 %collective-permute-start.43 = (bf16[48,2048]{1,0:T(8,128)(2,1)S(1)}, bf16[48,2048]{1,0:T(8,128)(2,1)S(1)}, u32[]{:S(2)}, u32[]{:S(2)}) collective-permute-start(bf16[48,2048]{1,0:T(8,128)(2,1)S(1)} %bitcast.60), channel_id=1, source_target_pairs={{0,80},{16,96},{32,112},{48,0},{64,16},{80,32},{96,48},{112,64},{1... | collective-permute-start | bytes 589832 | tf_op jit(solution)/shard_map/ppermute | solution.py:309
  364.6 17.3 %collective-permute-start.42 = (bf16[48,2048]{1,0:T(8,128)(2,1)S(1)}, bf16[48,2048]{1,0:T(8,128)(2,1)S(1)}, u32[]{:S(2)}, u32[]{:S(2)}) collective-permute-start(bf16[48,2048]{1,0:T(8,128)(2,1)S(1)} %bitcast.59), channel_id=1, source_target_pairs={{0,64},{16,80},{32,96},{48,112},{64,0},{80,16},{96,32},{112,48},{1... | collective-permute-start | bytes 589832 | tf_op jit(solution)/shard_map/ppermute | solution.py:309
  371.4 10.5 %collective-permute-start.41 = (bf16[48,2048]{1,0:T(8,128)(2,1)S(1)}, bf16[48,2048]{1,0:T(8,128)(2,1)S(1)}, u32[]{:S(2)}, u32[]{:S(2)}) collective-permute-start(bf16[48,2048]{1,0:T(8,128)(2,1)S(1)} %bitcast.58), channel_id=1, source_target_pairs={{0,48},{16,64},{32,80},{48,96},{64,112},{80,0},{96,16},{112,32},{1... | collective-permute-start | bytes 589832 | tf_op jit(solution)/shard_map/ppermute | solution.py:309
  372.1 12.9 %collective-permute-start.40 = (bf16[48,2048]{1,0:T(8,128)(2,1)S(1)}, bf16[48,2048]{1,0:T(8,128)(2,1)S(1)}, u32[]{:S(2)}, u32[]{:S(2)}) collective-permute-start(bf16[48,2048]{1,0:T(8,128)(2,1)S(1)} %bitcast.57), channel_id=1, source_target_pairs={{0,32},{16,48},{32,64},{48,80},{64,96},{80,112},{96,0},{112,16},{1... | collective-permute-start | bytes 589832 | tf_op jit(solution)/shard_map/ppermute | solution.py:309
  372.5 15.0 %collective-permute-start.39 = (bf16[48,2048]{1,0:T(8,128)(2,1)S(1)}, bf16[48,2048]{1,0:T(8,128)(2,1)S(1)}, u32[]{:S(2)}, u32[]{:S(2)}) collective-permute-start(bf16[48,2048]{1,0:T(8,128)(2,1)S(1)} %bitcast.56), channel_id=1, source_target_pairs={{0,16},{16,32},{32,48},{48,64},{64,80},{80,96},{96,112},{112,0},{1... | collective-permute-start | bytes 589832 | tf_op jit(solution)/shard_map/ppermute | solution.py:309
  394.0 32.2 %collective-permute-start.53 = (bf16[512,1024]{1,0:T(8,128)(2,1)S(1)}, bf16[512,1024]{1,0:T(8,128)(2,1)S(1)}, u32[]{:S(2)}, u32[]{:S(2)}) collective-permute-start(bf16[512,1024]{1,0:T(8,128)(2,1)S(1)} %get-tuple-element.401), channel_id=1, source_target_pairs={{0,8},{8,0},{1,9},{9,1},{2,10},{10,2},{3,11},{11,3},{4,12},{12,4},... | collective-permute-start | bytes 3145736 | tf_op jit(solution)/shard_map/ppermute | solution.py:340
  (26 other events, 195.2 us)
